TPU v7x, 128 devices: a whole 4x4x4 slice. The times are simulated.
128 devices in a mesh: req: 4 (over x), exp: 32 (over y, z, core).
Axes of the slice: x: 4, y: 4, z: 4, core: 2. Of those that a mesh axis runs over, the one named last changes fastest.
Arguments:
- tokens: bfloat16 [32768, 1536], P(('req', 'exp')), may hold values from -6 to 6
- token_request_slot: int32 [128, 256], P(('req', 'exp')), may hold values from 0 to 3, never falling along the last dimension, each value on 1 to 128 neighbouring positions
- request_prompt: int32 [512], P(('req', 'exp')), may hold values from 0 to 31
- request_adapter: int32 [512], P(('req', 'exp')), may hold values from 0 to 15
- prompt_page_table: int32 [512], replicated, may hold values from 0 to 511, each once
- shared_prompt_cache: bfloat16 [512, 16, 512], P(('req', 'exp')), may hold values from -180 to 180
- routes: int32 [32768, 4], P(('req', 'exp')), may hold values from 0 to 31, all different within a row; in each aligned block of 256 rows (0 to 255, 256 to 511, ...) at most 48 rows name the same one
- attention_norm_gain: bfloat16 [1536], replicated, may hold values from 0.099609375 to 1.8984375
- query_matrix: bfloat16 [1536, 1536], replicated, may hold values from -0.15625 to 0.15625
- key_value_weight: bfloat16 [1536, 512], replicated, may hold values from -0.15625 to 0.15625
- attention_output_weight: bfloat16 [1536, 1536], replicated, may hold values from -0.15625 to 0.15625
- adapter_query_down: bfloat16 [1536, 256], replicated, may hold values from -0.15625 to 0.15625
- adapter_query_up: bfloat16 [256, 1536], replicated, may hold values from -1.5 to 1.5
- adapter_output_down: bfloat16 [1536, 256], replicated, may hold values from -0.15625 to 0.15625
- adapter_output_up: bfloat16 [256, 1536], replicated, may hold values from -1.5 to 1.5
- expert_norm_gain: bfloat16 [1536], replicated, may hold values from 0.099609375 to 1.8984375
- router: bfloat16 [1536, 32], replicated, may hold values from -0.15625 to 0.15625
- expert_gate_up: bfloat16 [32, 1536, 1536], P('exp'), may hold values from -0.15625 to 0.15625
- expert_down: bfloat16 [32, 768, 1536], P('exp'), may hold values from -0.21875 to 0.21875
Outputs:
- mixed_rows: bfloat16 [32768, 1536], P(('req', 'exp'))
Inputs may be any that keep to these rules, and one draw needn't show every extreme that they name: `token_request_slot`: along a device's row the slots never fall; each of the 4 slots holds 1 to 128 tokens and one holds exactly 128. `prompt_page_table`: the entries whose index divided by 16 (rounded down) is p are the pages of prompt p in order; every page appears once. `routes`: each token names 4 different experts. Among the tokens of one device no expert is named more than 48 times, and in every draw some device's tokens name some expert exactly 48 times.
All inputs are finite; a program needn't handle non-finite values.
Results may differ from a plain program's by a relative error of at most 0.017.
The roundings to bfloat16 on the way count: a program that leaves them out, or rounds other values in their place, can miss the bound.
Values may be sent and summed in bfloat16 or wider, within the bound.
A program may use at most 128 MiB of HBM per device.

v0:
```python
import jax
import jax.numpy as jnp
from jax import lax
from jax.sharding import PartitionSpec as P

QUERY_HEADS = 12
KEY_VALUE_HEADS = 2
HEAD_WIDTH = 128
TOPK = 4
ADAPTER_RANK = 16
PPP = 16
PROMPT_LENGTH = 256


EPSILON = 1e-06
THETA = 1000000.0
VERY_NEGATIVE = -1e30


def rms_norm(weight_matrix, gain_vector):
    values = weight_matrix.astype(jnp.float32)
    factor = lax.rsqrt(jnp.mean(values * values, axis=-1, keepdims=True) + EPSILON)
    return (values * factor * gain_vector.astype(jnp.float32)).astype(jnp.bfloat16)


def apply_rotary(values, token_positions):
    half_width = values.shape[-1] // 2
    frequency = THETA ** (-jnp.arange(half_width).astype(jnp.float32) / half_width)
    angles = token_positions.astype(jnp.float32)[:, None] * frequency[None, :]
    cosine = jnp.cos(angles)[:, None, :]
    sine_table = jnp.sin(angles)[:, None, :]
    first_half = values[..., :half_width]
    second = values[..., half_width:]
    return jnp.concatenate(
        [first_half * cosine - second * sine_table, second * cosine + first_half * sine_table],
        axis=-1,
    )


def adapter_update(weight_matrix, down_proj, up_proj, token_adapter):
    inner = jnp.dot(weight_matrix, down_proj, preferred_element_type=jnp.float32)
    owner_slot = jnp.arange(down_proj.shape[1], dtype=jnp.int32) // ADAPTER_RANK
    inner = jnp.where(owner_slot[None, :] == token_adapter[:, None], inner, 0.0).astype(
        jnp.bfloat16
    )
    return jnp.dot(inner, up_proj, preferred_element_type=jnp.float32)


def request_info(request_row, prompt_req, adapter_req):
    new_token_count = request_row.shape[0]
    request_slot_count = prompt_req.shape[0]
    matches = request_row[:, None] == jnp.arange(request_slot_count, dtype=jnp.int32)[None, :]
    token_adapter = jnp.sum(jnp.where(matches, adapter_req[None, :], 0), axis=1)
    prompt_tok = jnp.sum(jnp.where(matches, prompt_req[None, :], 0), axis=1)
    token_index = jnp.arange(new_token_count, dtype=jnp.int32)
    first_row = jnp.min(jnp.where(matches, token_index[:, None], new_token_count), axis=0)
    start_tok = jnp.sum(jnp.where(matches, first_row[None, :], 0), axis=1)
    token_positions = PROMPT_LENGTH + token_index - start_tok
    return (token_adapter, prompt_tok, token_positions)


def apply_projection(
    tokens,
    token_adapter,
    token_positions,
    attention_norm_gain,
    query_matrix,
    key_value_weight,
    adapter_query_down,
    adapter_query_up,
):
    new_token_count = tokens.shape[0]
    normalized = rms_norm(tokens, attention_norm_gain)
    query_rows = jnp.dot(normalized, query_matrix, preferred_element_type=jnp.float32)
    query_rows = query_rows + adapter_update(
        normalized, adapter_query_down, adapter_query_up, token_adapter
    )
    query_rows = apply_rotary(
        query_rows.reshape(new_token_count, QUERY_HEADS, HEAD_WIDTH), token_positions
    ).astype(jnp.bfloat16)
    key_value_rows = jnp.dot(
        normalized, key_value_weight, preferred_element_type=jnp.float32
    ).reshape(new_token_count, 2 * KEY_VALUE_HEADS, HEAD_WIDTH)
    key_matrix = apply_rotary(key_value_rows[:, :KEY_VALUE_HEADS], token_positions).astype(
        jnp.bfloat16
    )
    value_matrix = key_value_rows[:, KEY_VALUE_HEADS:].astype(jnp.bfloat16)
    return (query_rows, key_matrix, value_matrix)


def finalize(
    attention_output,
    tokens,
    token_adapter,
    attention_output_weight,
    adapter_output_down,
    adapter_output_up,
):
    expert_mixture = jnp.dot(
        attention_output, attention_output_weight, preferred_element_type=jnp.float32
    )
    expert_mixture = expert_mixture + adapter_update(
        attention_output, adapter_output_down, adapter_output_up, token_adapter
    )
    return (tokens.astype(jnp.float32) + expert_mixture).astype(jnp.bfloat16)


def gate_weights(ffn_normed, router, routes):
    logits = jnp.dot(ffn_normed, router, preferred_element_type=jnp.float32)
    picked = jnp.take_along_axis(logits, routes, axis=1)
    squashed = jax.nn.sigmoid(picked)
    return squashed / jnp.sum(squashed, axis=1, keepdims=True)


def slot_of(routes, experts, capacity):
    flat_routes = routes.reshape(-1)
    onehot = (flat_routes[:, None] == jnp.arange(experts, dtype=jnp.int32)[None, :]).astype(
        jnp.int32
    )
    before = jnp.cumsum(onehot, axis=0) - onehot
    rank_pick = jnp.sum(before * onehot, axis=1)
    return flat_routes * capacity + rank_pick


def block_attention(running, grouped_queries, key_matrix, value_matrix, allowed):
    running_max, totals, accum = running
    scale = grouped_queries.shape[-1] ** (-0.5)
    scores = (
        jnp.einsum(
            "tkgd,nkd->tkgn", grouped_queries, key_matrix, preferred_element_type=jnp.float32
        )
        * scale
    )
    scores = jnp.where(allowed[:, None, None, :], scores, VERY_NEGATIVE)
    new_max = jnp.maximum(running_max, jnp.max(scores, axis=-1))
    factor = jnp.exp(running_max - new_max)
    weights = jnp.exp(scores - new_max[..., None])
    totals = totals * factor + jnp.sum(weights, axis=-1)
    summed = jnp.einsum(
        "tkgn,nkd->tkgd",
        weights.astype(jnp.bfloat16),
        value_matrix,
        preferred_element_type=jnp.float32,
    )
    accum = accum * factor[..., None] + summed
    return (new_max, totals, accum)


def on_device(
    tokens,
    token_request_slot,
    request_prompt,
    request_adapter,
    prompt_page_table,
    shared_prompt_cache,
    routes,
    attention_norm_gain,
    query_matrix,
    key_value_weight,
    attention_output_weight,
    adapter_query_down,
    adapter_query_up,
    adapter_output_down,
    adapter_output_up,
    expert_norm_gain,
    router,
    expert_gate_up,
    expert_down,
):
    new_token_count = tokens.shape[0]
    request_row = token_request_slot[0]
    request_slot_count = request_prompt.shape[0]
    token_adapter, prompt_tok, token_positions = request_info(
        request_row, request_prompt, request_adapter
    )
    query_rows, key_matrix, value_matrix = apply_projection(
        tokens,
        token_adapter,
        token_positions,
        attention_norm_gain,
        query_matrix,
        key_value_weight,
        adapter_query_down,
        adapter_query_up,
    )
    query_group_width = QUERY_HEADS // KEY_VALUE_HEADS
    grouped_queries = query_rows.reshape(
        new_token_count, KEY_VALUE_HEADS, query_group_width, HEAD_WIDTH
    )
    token_index = jnp.arange(new_token_count, dtype=jnp.int32)
    local_ok = (request_row[:, None] == request_row[None, :]) & (
        token_index[None, :] <= token_index[:, None]
    )
    initial = (
        jnp.full((new_token_count, KEY_VALUE_HEADS, query_group_width), VERY_NEGATIVE, jnp.float32),
        jnp.zeros((new_token_count, KEY_VALUE_HEADS, query_group_width), jnp.float32),
        jnp.zeros((new_token_count, KEY_VALUE_HEADS, query_group_width, HEAD_WIDTH), jnp.float32),
    )
    running_progress = block_attention(initial, grouped_queries, key_matrix, value_matrix, local_ok)
    requested_pages = jnp.take(prompt_page_table.reshape(-1, PPP), request_prompt, axis=0).reshape(
        -1
    )
    complete_cache = lax.all_gather(shared_prompt_cache, ("req", "exp"), axis=0, tiled=True)
    page_token_rows = jnp.take(complete_cache, requested_pages, axis=0).reshape(
        request_slot_count * PROMPT_LENGTH, 2 * KEY_VALUE_HEADS, HEAD_WIDTH
    )
    owner_slot = jnp.arange(request_slot_count * PROMPT_LENGTH, dtype=jnp.int32) // PROMPT_LENGTH
    prompt_valid_mask = request_row[:, None] == owner_slot[None, :]
    running_progress = block_attention(
        running_progress,
        grouped_queries,
        page_token_rows[:, :KEY_VALUE_HEADS],
        page_token_rows[:, KEY_VALUE_HEADS:],
        prompt_valid_mask,
    )
    running_max, totals, accum = running_progress
    attention_output = (
        (accum / totals[..., None])
        .reshape(new_token_count, QUERY_HEADS * HEAD_WIDTH)
        .astype(jnp.bfloat16)
    )
    hidden_state = finalize(
        attention_output,
        tokens,
        token_adapter,
        attention_output_weight,
        adapter_output_down,
        adapter_output_up,
    )
    ffn_normed = rms_norm(hidden_state, expert_norm_gain)
    gates = gate_weights(ffn_normed, router, routes)
    local_experts = expert_gate_up.shape[0]
    experts = local_experts * lax.axis_size("exp")
    capacity = 3 * new_token_count * TOPK // (2 * experts)
    destination = slot_of(routes, experts, capacity)
    slot_total = experts * capacity
    matches = jnp.arange(slot_total, dtype=jnp.int32)[:, None] == destination[None, :]
    source = jnp.arange(new_token_count * TOPK, dtype=jnp.int32) // TOPK
    source_tok = jnp.sum(jnp.where(matches, source[None, :], 0), axis=1)
    filled = jnp.any(matches, axis=1)
    outgoing = jnp.where(
        filled[:, None], jnp.take(ffn_normed, source_tok, axis=0), jnp.zeros((), jnp.bfloat16)
    )
    outgoing = outgoing.reshape(experts, capacity, -1)
    arrived = lax.all_to_all(outgoing, "exp", split_axis=0, concat_axis=0, tiled=True)
    sources = arrived.shape[0] // local_experts
    item_count = arrived.shape[1]
    arranged = arrived.reshape(sources, local_experts, item_count, -1)
    inner = jnp.einsum(
        "sxcd,xdf->sxcf", arranged, expert_gate_up, preferred_element_type=jnp.float32
    )
    half_width = inner.shape[-1] // 2
    units = (jax.nn.relu(inner[..., :half_width]) * inner[..., half_width:]).astype(jnp.bfloat16)
    result = jnp.einsum(
        "sxcf,xfd->sxcd", units, expert_down, preferred_element_type=jnp.float32
    ).astype(jnp.bfloat16)
    result = result.reshape(sources * local_experts, item_count, -1)
    returned = lax.all_to_all(result, "exp", split_axis=0, concat_axis=0, tiled=True)
    picked = jnp.take(returned.reshape(slot_total, -1), destination, axis=0).astype(jnp.float32)
    picked = picked.reshape(new_token_count, TOPK, -1)
    mixed_rows = hidden_state.astype(jnp.float32) + jnp.sum(gates[..., None] * picked, axis=1)
    return mixed_rows.astype(jnp.bfloat16)


def solution(mesh):
    return jax.shard_map(
        on_device,
        mesh=mesh,
        in_specs=(
            P(("req", "exp"), None),
            P(("req", "exp"), None),
            P(("req", "exp")),
            P(("req", "exp")),
            P(),
            P(("req", "exp"), None, None),
            P(("req", "exp"), None),
            P(),
            P(),
            P(),
            P(),
            P(),
            P(),
            P(),
            P(),
            P(),
            P(),
            P("exp", None, None),
            P("exp", None, None),
        ),
        out_specs=P(("req", "exp"), None),
        check_vma=False,
    )
```

profile of v0, /device:TPU:1, one launch (start us, length us, event | category | flops | bytes accessed | tf_op | source)
XLA Modules:
  0.0 307.1 jit_solution(16378191095570078321)
XLA Ops:
  14.4 9.0 %reduce-window.6 = s32[32,8,128]{2,1,0:T(8,128)S(1)} reduce-window(s32[32,8,128]{2,1,0:T(8,128)S(1)} %fusion.53, s32[]{:T(128)} %constant.133.clone.1), window={size=1x1x128 pad=0_0x0_0x127_0}, to_apply=%region_10.11 | reduce-window | flops 4161536 | bytes 262148 | tf_op jit(solution)/shard_map/reduce-window
  31.6 2.8 fusion.75
  38.4 4.9 %fusion.73 = f32[256,1536]{1,0:T(8,128)} fusion(bf16[1536,1536]{1,0:T(8,128)(2,1)} %param.27, bf16[256,1536]{1,0:T(8,128)(2,1)S(1)} %copy-done.4, f32[1536]{0:T(1024)S(1)} %convert_element_type.85, f32[256]{0:T(256)S(1)} %add_rsqrt_fusion.1), kind=kOutput, calls=%fused_computation.157 | convolution fusion | flops 1209532416 | bytes 7085056 | tf_op jit(solution)/shard_map/dot_general | solution.py:74
  43.3 4.2 %convolution_add_fusion.1 = f32[256,1536]{1,0:T(8,128)} fusion(f32[256,1536]{1,0:T(8,128)} %fusion.73, bf16[256,1536]{1,0:T(8,128)(2,1)} %param.31, bf16[1536,256]{1,0:T(8,128)(2,1)} %param.30, s32[256]{0:T(256)S(1)} %and_select_fusion, s32[256]{0:T(256)S(1)} %get-tuple-element.5, bf16[256,1536]{1,0:T(8,128)(2,1)S(1)} %copy-done.4, ...), kind=kOutput, calls=%fused_computation.27 | convolution fusion | flops 404815872 | bytes 5514240 | tf_op jit(solution)/shard_map/dot_general | solution.py:46
  47.5 3.2 %copy.100 = f32[256,1536]{0,1:T(8,128)} copy(f32[256,1536]{1,0:T(8,128)} %convolution_add_fusion.1) | data formatting | bytes 3145728 | tf_op jit(solution)/shard_map/add | solution.py:75
  61.3 3.9 %fusion.14 = (f32[256,2,6]{0,2,1:T(8,128)S(1)}, f32[2,256,256,6]{2,1,3,0:T(8,128)}) fusion(pred[256,256]{0,1:T(8,128)(4,1)S(1)} %fusion.38, bf16[256,2,6,64]{3,0,2,1:T(8,128)(2,1)} %bitcast.121, bf16[256,2,6,64]{3,0,2,1:T(8,128)(2,1)S(1)} %bitcast.119, bf16[256,2,64]{2,0,1:T(8,128)(2,1)S(1)} %get-tuple-element.14, bf16[256,2,64]{2,0,1:T(8,128)(2,1)S(1)} %get-tuple-element.13), kind=kOutput, calls=%fused_computation.32 | convolution fusion | flops 205517824 | bytes 4141056 | tf_op jit(solution)/shard_map/tkgd,nkd->tkgn/dot_general | solution.py:129
  65.2 19.0 %all-gather.2.cloned.1.call-done = bf16[512,16,512]{2,1,0:T(8,128)(2,1)} async-done(((bf16[4,16,512]{2,1,0:T(8,128)(2,1)}), bf16[512,16,512]{2,1,0:T(8,128)(2,1)}) %all-gather.2.cloned.1.call-update) | async-done | bytes 8388624 | tf_op jit(solution)/shard_map/all_gather | solution.py:203
  84.2 5.0 %gather_fusion.1 = bf16[64,16,512]{2,1,0:T(8,128)(2,1)} fusion(bf16[512,16,512]{2,1,0:T(8,128)(2,1)} %all-gather.2.cloned.1.call-done, s32[1024]{0:T(1024)S(1)} %pad_clamp_fusion.1), kind=kCustom, calls=%fused_computation.1 | custom fusion | bytes 2097408 | tf_op jit(solution)/shard_map/jit(_take)/gather | solution.py:204
  92.8 3.8 %fusion.2 = (f32[256,2,6]{0,2,1:T(8,128)S(1)}, f32[2,1024,256,6]{2,1,3,0:T(8,128)S(1)}) fusion(pred[256,1024]{0,1:T(8,128)(4,1)S(1)} %broadcast_compare_fusion, bf16[256,2,6,64]{3,0,2,1:T(8,128)(2,1)} %bitcast.122, bf16[256,2,6,64]{3,0,2,1:T(8,128)(2,1)S(1)} %bitcast.120, bf16[1024,4,128]{2,0,1:T(8,128)(2,1)S(1)} %copy_select_fusion), kind=kOutput, calls=%fused_computation.9 | convolution fusion | flops 816313344 | bytes 14561280 | tf_op jit(solution)/shard_map/tkgd,nkd->tkgn/dot_general | solution.py:129
  99.6 2.5 fusion
  102.1 4.4 %fusion.25 = bf16[256,2,6,128]{0,3,2,1:T(8,128)(2,1)S(1)} fusion(f32[2,128,256,6]{2,1,3,0:T(8,128)} %fusion.22, f32[2,1024,256,6]{2,1,3,0:T(8,128)S(1)} %get-tuple-element.25, f32[256,2,6]{0,2,1:T(8,128)S(1)} %get-tuple-element.18, pred[256,1024]{0,1:T(8,128)(4,1)S(1)} %broadcast_compare_fusion, f32[256,2,6]{0,2,1:T(8,128)S(1)} %get-tuple-element.9, ...), kind=kOutput, calls=%fused_computation.44 | convolution fusion | flops 819855360 | bytes 15794176 | tf_op jit(solution)/shard_map/tkgn,nkd->tkgd/dot_general | solution.py:139
  107.4 5.0 %fusion.78 = f32[256,1536]{1,0:T(8,128)} fusion(bf16[256,1536]{0,1:T(8,128)(2,1)S(1)} %bitcast.124, bf16[1536,1536]{1,0:T(8,128)(2,1)} %param.29), kind=kOutput, calls=%fused_computation.160 | convolution fusion | flops 1207959552 | bytes 7077888 | tf_op jit(solution)/shard_map/dot_general | solution.py:99
  112.4 4.3 %multiply_reduce_fusion.1 = (f32[256]{0:T(256)S(1)}, f32[256,1536]{1,0:T(8,128)}) fusion(f32[256,1536]{1,0:T(8,128)} %fusion.78, bf16[256,1536]{1,0:T(8,128)(2,1)} %param.33, bf16[256,1536]{0,1:T(8,128)(2,1)} %bitcast.125, bf16[1536,256]{1,0:T(8,128)(2,1)} %param.32, s32[256]{0:T(256)S(1)} %copy-done.23, s32[256]{0:T(256)S(1)} %copy-done.20, ...), kind=kOutput, calls=%fused_computation.49 | convolution fusion | flops 405602048 | bytes 6294528 | tf_op jit(solution)/shard_map/dot_general | solution.py:46
  118.4 6.2 %gather_fusion.2 = bf16[1536,1536]{1,0:T(8,128)(2,1)} fusion(bf16[256,1536]{1,0:T(8,128)(2,1)S(1)} %multiply_convert_fusion, s32[2048]{0:T(1024)S(1)} %pad_clamp_fusion), kind=kCustom, calls=%fused_computation.2 | custom fusion | bytes 9443328 | tf_op jit(solution)/shard_map/jit(_take)/gather | solution.py:242
  124.6 2.8 select_select_fusion
  127.4 61.1 %all_to_all.10 = bf16[32,48,1536]{2,1,0:T(8,128)(2,1)S(1)} all-to-all(bf16[32,48,1536]{2,1,0:T(8,128)(2,1)S(1)} %select_select_fusion), channel_id=1, replica_groups=mesh['req'=4,'exp'=32] {'exp'}, dimensions={0} | all-to-all | bytes 9437184 | tf_op jit(solution)/shard_map/all_to_all | solution.py:245
  188.5 9.7 %convolution_bitcast_fusion = f32[32,1,48,1536]{3,2,0,1:T(8,128)S(1)} fusion(bf16[32,48,1536]{2,1,0:T(8,128)(2,1)S(1)} %all_to_all.10, bf16[1,1536,1536]{2,1,0:T(8,128)(2,1)} %param.36), kind=kOutput, calls=%fused_computation.16 | convolution fusion | flops 7247757312 | bytes 18874368 | tf_op jit(solution)/shard_map/sxcd,xdf->sxcf/dot_general | solution.py:249
  198.2 5.5 %convolution_convert_fusion = bf16[32,48,1536]{2,1,0:T(8,128)(2,1)} fusion(f32[32,1,48,1536]{3,2,0,1:T(8,128)S(1)} %convolution_bitcast_fusion, bf16[1,768,1536]{2,1,0:T(8,128)(2,1)S(1)} %copy-done), kind=kOutput, calls=%fused_computation.22 | convolution fusion | flops 3629776896 | bytes 16515072 | tf_op jit(solution)/shard_map/sxcf,xfd->sxcd/dot_general | solution.py:254
  203.7 4.8 %all-to-all-start.1 = ((bf16[32,48,1536]{2,1,0:T(8,128)(2,1)}), bf16[32,48,1536]{2,1,0:T(8,128)(2,1)}, u32[]{:S(2)}, u32[]{:S(2)}) async-start(bf16[32,48,1536]{2,1,0:T(8,128)(2,1)} %convolution_convert_fusion), calls=%async_computation.1 | async-start | bytes 9437184 | tf_op jit(solution)/shard_map/all_to_all | solution.py:258
  209.8 8.7 %gather_fusion.4 = f32[1024]{0:T(1024)S(1)} fusion(f32[256,32]{0,1:T(8,128)S(1)} %fusion.79, s32[1024]{0:T(1024)S(1)} %reshape.466), kind=kCustom, calls=%fused_computation.4 | custom fusion | bytes 16384 | tf_op jit(solution)/shard_map/jit(take_along_axis)/gather | solution.py:110
  218.9 47.7 %all-to-all-done.1 = bf16[32,48,1536]{2,1,0:T(8,128)(2,1)} async-done(((bf16[32,48,1536]{2,1,0:T(8,128)(2,1)}), bf16[32,48,1536]{2,1,0:T(8,128)(2,1)}, u32[]{:S(2)}, u32[]{:S(2)}) %all-to-all-start.1) | async-done | bytes 4718624 | tf_op jit(solution)/shard_map/all_to_all | solution.py:258
  266.6 10.2 %gather_fusion.3 = bf16[1024,1536]{1,0:T(8,128)(2,1)} fusion(bf16[1536,1536]{1,0:T(8,128)(2,1)} %bitcast.31, s32[1024]{0:T(1024)S(1)} %broadcast_clamp_fusion), kind=kCustom, calls=%fused_computation.3 | custom fusion | bytes 6295552 | tf_op jit(solution)/shard_map/jit(_take)/gather | solution.py:259
  276.9 6.1 %gather.33 = bf16[256,4,1536]{2,1,0:T(4,128)(2,1)} reshape(bf16[1024,1536]{1,0:T(8,128)(2,1)} %gather_fusion.3) | data formatting | bytes 6291456 | tf_op jit(solution)/shard_map/jit(_take)/gather | solution.py:259
  283.0 16.2 %multiply_reduce_fusion = f32[256,1536]{1,0:T(8,128)S(1)} fusion(bf16[256,4,1536]{2,1,0:T(4,128)(2,1)} %gather.33, f32[256,4]{1,0:T(8,128)S(1)} %copy.110, pred[256,4]{1,0:T(8,128)(4,1)S(1)} %copy.116), kind=kLoop, calls=%fused_computation.10 | loop fusion | flops 5898240 | bytes 4723712 | tf_op jit(solution)/shard_map/reduce_sum | solution.py:261
  (132 shorter events, 42.2 us)
Async XLA Ops:
  6.5 191.7 %copy-start = (bf16[1,768,1536]{2,1,0:T(8,128)(2,1)S(1)}, bf16[1,768,1536]{2,1,0:T(8,128)(2,1)}, u32[]{:S(2)}) copy-start(bf16[1,768,1536]{2,1,0:T(8,128)(2,1)} %param.37) | copy-start | bytes 7077892
  6.5 25.1 %copy-start.4 = (bf16[256,1536]{1,0:T(8,128)(2,1)S(1)}, bf16[256,1536]{1,0:T(8,128)(2,1)}, u32[]{:S(2)}) copy-start(bf16[256,1536]{1,0:T(8,128)(2,1)} %param.19) | copy-start | bytes 2359300
  6.5 77.7 %all-gather.2.cloned.1.call-start = ((), (), s32[]{:S(2)}) async-start(), calls=%async_computation.2 | async-start | bytes 8454144 | tf_op jit(solution)/shard_map/all_gather | solution.py:203
  26.7 11.7 %copy-start.17 = (s32[1536]{0:T(1024)}, s32[1536]{0:T(1024)S(1)}, u32[]{:S(2)}) copy-start(s32[1536]{0:T(1024)S(1)} %select_reduce_fusion) | copy-start | bytes 18436
  28.4 14.9 %copy-start.19 = (s32[256]{0:T(256)}, s32[256]{0:T(256)S(1)}, u32[]{:S(2)}) copy-start(s32[256]{0:T(256)S(1)} %get-tuple-element.5) | copy-start | bytes 3076
  28.7 14.6 %copy-start.7 = (f32[256,64]{0,1:T(8,128)}, f32[256,64]{0,1:T(8,128)S(1)}, u32[]{:S(2)}) copy-start(f32[256,64]{0,1:T(8,128)S(1)} %get-tuple-element.20) | copy-start | bytes 196612
  28.8 14.6 %copy-start.9 = (f32[256,64]{0,1:T(8,128)}, f32[256,64]{0,1:T(8,128)S(1)}, u32[]{:S(2)}) copy-start(f32[256,64]{0,1:T(8,128)S(1)} %get-tuple-element.21) | copy-start | bytes 196612
  38.4 4.9 %copy-start.22 = (s32[256]{0:T(256)}, s32[256]{0:T(256)S(1)}, u32[]{:S(2)}) copy-start(s32[256]{0:T(256)S(1)} %and_select_fusion) | copy-start | bytes 3076
  47.5 3.2 %copy-start.8 = (f32[256,64]{0,1:T(8,128)S(1)}, f32[256,64]{0,1:T(8,128)}, u32[]{:S(2)}) copy-start(f32[256,64]{0,1:T(8,128)} %copy-done.7) | copy-start | bytes 196612
  47.5 3.2 %copy-start.10 = (f32[256,64]{0,1:T(8,128)S(1)}, f32[256,64]{0,1:T(8,128)}, u32[]{:S(2)}) copy-start(f32[256,64]{0,1:T(8,128)} %copy-done.9) | copy-start | bytes 196612
  65.2 26.1 %copy-start.21 = (pred[1024]{0:T(1024)(128)(4,1)S(1)}, pred[1024]{0:T(1024)(128)(4,1)}, u32[]{:S(2)}) copy-start(pred[1024]{0:T(1024)(128)(4,1)} %broadcast_in_dim.194) | copy-start | bytes 3076
  92.8 3.9 %copy-start.2 = (f32[2,256,256,6]{2,1,3,0:T(8,128)S(1)}, f32[2,256,256,6]{2,1,3,0:T(8,128)}, u32[]{:S(2)}) copy-start(f32[2,256,256,6]{2,1,3,0:T(8,128)} %get-tuple-element.23) | copy-start | bytes 9437188
  96.6 0.9 copy-start.11
  107.4 5.0 %copy-start.5 = (bf16[256,1536]{1,0:T(8,128)(2,1)S(1)}, bf16[256,1536]{1,0:T(8,128)(2,1)}, u32[]{:S(2)}) copy-start(bf16[256,1536]{1,0:T(8,128)(2,1)} %param.19) | copy-start | bytes 2359300
  107.4 5.0 %copy-start.20 = (s32[256]{0:T(256)S(1)}, s32[256]{0:T(256)}, u32[]{:S(2)}) copy-start(s32[256]{0:T(256)} %copy-done.19) | copy-start | bytes 3076
  107.4 5.0 %copy-start.23 = (s32[256]{0:T(256)S(1)}, s32[256]{0:T(256)}, u32[]{:S(2)}) copy-start(s32[256]{0:T(256)} %copy-done.22) | copy-start | bytes 3076
  112.4 4.4 %copy-start.16 = (f32[1536]{0:T(1024)S(1)}, f32[1536]{0:T(1024)}, u32[]{:S(2)}) copy-start(f32[1536]{0:T(1024)} %convert_element_type.97) | copy-start | bytes 18436
  118.4 6.2 %copy-start.18 = (pred[32,48]{1,0:T(8,128)(4,1)S(1)}, pred[32,48]{1,0:T(8,128)(4,1)}, u32[]{:S(2)}) copy-start(pred[32,48]{1,0:T(8,128)(4,1)} %broadcast_in_dim.200) | copy-start | bytes 4612
  203.7 4.8 %copy-start.15 = (s32[1024]{0:T(1024)S(1)}, s32[1024]{0:T(1024)}, u32[]{:S(2)}) copy-start(s32[1024]{0:T(1024)} %copy-done.14) | copy-start | bytes 12292
  203.7 4.9 %copy-start.12 = (s32[256,4]{0,1:T(4,128)S(1)}, s32[256,4]{0,1:T(4,128)}, u32[]{:S(2)}) copy-start(s32[256,4]{0,1:T(4,128)} %param.25) | copy-start | bytes 12292
  203.7 5.8 %copy-start.13 = (bf16[1536,32]{0,1:T(8,128)(2,1)S(1)}, bf16[1536,32]{0,1:T(8,128)(2,1)}, u32[]{:S(2)}) copy-start(bf16[1536,32]{0,1:T(8,128)(2,1)} %param.35) | copy-start | bytes 294916
  203.7 62.9 %all-to-all-start.1 = ((bf16[32,48,1536]{2,1,0:T(8,128)(2,1)}), bf16[32,48,1536]{2,1,0:T(8,128)(2,1)}, u32[]{:S(2)}, u32[]{:S(2)}) async-start(bf16[32,48,1536]{2,1,0:T(8,128)(2,1)} %convolution_convert_fusion), calls=%async_computation.1 | async-start | bytes 9437184 | tf_op jit(solution)/shard_map/all_to_all | solution.py:258
  283.0 16.3 %copy-start.3 = (f32[256,1536]{1,0:T(8,128)S(1)}, f32[256,1536]{1,0:T(8,128)}, u32[]{:S(2)}) copy-start(f32[256,1536]{1,0:T(8,128)} %get-tuple-element.27) | copy-start | bytes 4718596
  283.0 17.3 %copy-start.1 = (bf16[1,768,1536]{2,1,0:T(8,128)(2,1)S(1)}, bf16[1,768,1536]{2,1,0:T(8,128)(2,1)}, u32[]{:S(2)}) copy-start(bf16[1,768,1536]{2,1,0:T(8,128)(2,1)} %param.37) | copy-start | bytes 7077892
  (2 other events, 1.5 us)
Sparse Core Ops, SparseCore 0:
  10.3 73.8 all-gather.1
where the time goes:
time: 312 us; the launch traced here: 307 us
  waiting for transfers between devices  67.4 us (22%)
  blocking collectives  61.1 us (20%)
  local copies, waits for them, and re-layouts  58.8 us (19%)
  matrix products  50.9 us (16%)
  other arithmetic  50.3 us (16%)
  between operations  13.9 us (4%)
  starting transfers between devices  4.77 us (2%)
    all_to_all x1, blocking collectives, on_device(): lax.all_to_all(outgoing, 'exp', split_axis=0, concat_axis=0, tiled=True)  61.1 us
    all_to_all x1, waiting for transfers between devices, on_device(): lax.all_to_all(result, 'exp', split_axis=0, concat_axis=0, tiled=True)  47.7 us
    all_gather x1, waiting for transfers between devices, on_device(): lax.all_gather(shared_prompt_cache, ('req', 'exp'), axis=0, tiled=True)  19 us
    gather x2, local copies, waits for them, and re-layouts, on_device(): jnp.take(returned.reshape(slot_total, -1), destination, axis=0)  16.3 us
    reduce_sum x1, other arithmetic, on_device(): jnp.sum(gates[..., None] * picked, axis=1)  16.2 us
    another operation x5, other arithmetic  12.5 us
    dot_general x1, matrix products, on_device(): jnp.einsum('sxcd,xdf->sxcf', arranged, expert_gate_up, preferred_element_...  9.72 us
    gather x5, local copies, waits for them, and re-layouts, gate_weights(): picked = jnp.take_along_axis(logits, routes, axis=1)  9.13 us
  transfers between devices with their start and end apart: 2, of which 2 were waited for; matrix products, arithmetic and copies ran while one was open for 22% of the time, Pallas kernels for 0%

commit v1 on v0

--- a/solution.py
+++ b/solution.py
@@ -1,7 +1,13 @@
 import jax
 import jax.numpy as jnp
 from jax import lax
+from jax.experimental import pallas as pl
+from jax.experimental.pallas import tpu as pltpu
 from jax.sharding import PartitionSpec as P
+
+MESH = pl.DeviceIdType.MESH
+CAP = 48
+FFE = 768
 
 QUERY_HEADS = 12
 KEY_VALUE_HEADS = 2
@@ -105,23 +111,6 @@
     return (tokens.astype(jnp.float32) + expert_mixture).astype(jnp.bfloat16)
 
 
-def gate_weights(ffn_normed, router, routes):
-    logits = jnp.dot(ffn_normed, router, preferred_element_type=jnp.float32)
-    picked = jnp.take_along_axis(logits, routes, axis=1)
-    squashed = jax.nn.sigmoid(picked)
-    return squashed / jnp.sum(squashed, axis=1, keepdims=True)
-
-
-def slot_of(routes, experts, capacity):
-    flat_routes = routes.reshape(-1)
-    onehot = (flat_routes[:, None] == jnp.arange(experts, dtype=jnp.int32)[None, :]).astype(
-        jnp.int32
-    )
-    before = jnp.cumsum(onehot, axis=0) - onehot
-    rank_pick = jnp.sum(before * onehot, axis=1)
-    return flat_routes * capacity + rank_pick
-
-
 def block_attention(running, grouped_queries, key_matrix, value_matrix, allowed):
     running_max, totals, accum = running
     scale = grouped_queries.shape[-1] ** (-0.5)
@@ -144,6 +133,258 @@
     )
     accum = accum * factor[..., None] + summed
     return (new_max, totals, accum)
+
+
+def moe_kernel(
+    hid_ref, gain_ref, routes_ref, router_ref, wgu_ref, wdn_ref,
+    out_ref,
+    xbuf, rbuf, rank_s, gate_s, ct_s, pack, arrived, units, result, returned,
+    psend, precv, acc,
+    sa_x, ra_x, sa_r, ra_r, sb_p, rb_p, sb_r, rb_r, sp_s, sp_r,
+):
+    x = lax.axis_index("req")
+    e_me = lax.axis_index("exp")
+    y = e_me // 8
+    z = lax.rem(e_me // 2, 4)
+    c = lax.rem(e_me, 2)
+    me_exp = e_me
+    first_pos = y * (1 - c) + z * c
+    first_base = z * 2 * (1 - c) + y * 8 * c + c
+    first_step = 8 - 6 * c
+    second_pos = z * (1 - c) + y * c
+    second_base = y * 8 * (1 - c) + z * 2 * c
+    second_step = 2 + 6 * c
+
+    def first_dev(offset):
+        return (x, first_base + lax.rem(first_pos + offset, 4) * first_step)
+
+    def second_exp(offset, dc):
+        return second_base + lax.rem(second_pos + offset, 4) * second_step + lax.rem(c + dc, 2)
+
+    def relay_dev(j, dc):
+        rc = lax.rem(c + dc, 2)
+        pos = z * (1 - rc) + y * rc
+        base = y * 8 * (1 - rc) + z * 2 * rc
+        return (x, base + lax.rem(pos - j + 4, 4) * (2 + 6 * rc) + rc)
+
+    def remote(src, dst, ssem, rsem, dev):
+        return pltpu.make_async_remote_copy(
+            src_ref=src, dst_ref=dst, send_sem=ssem, recv_sem=rsem,
+            device_id=dev, device_id_type=MESH)
+
+    barrier = pltpu.get_barrier_semaphore()
+    for dy in range(4):
+        for dc in range(2):
+            if dy or dc:
+                dev = (x, (lax.rem(y + dy, 4) * 4 + z) * 2 + lax.rem(c + dc, 2))
+                pl.semaphore_signal(barrier, 1, device_id=dev, device_id_type=MESH)
+    for dz in range(1, 4):
+        for dc in range(2):
+            dev = (x, (y * 4 + lax.rem(z + dz, 4)) * 2 + lax.rem(c + dc, 2))
+            pl.semaphore_signal(barrier, 1, device_id=dev, device_id_type=MESH)
+
+    hv = hid_ref[...].astype(jnp.float32)
+    factor = lax.rsqrt(jnp.mean(hv * hv, axis=-1, keepdims=True) + EPSILON)
+    xbuf[0] = (hv * factor * gain_ref[...].astype(jnp.float32)).astype(jnp.bfloat16)
+    rbuf[0] = routes_ref[...]
+    acc[...] = hv
+    pl.semaphore_wait(barrier, 13)
+
+    half = xbuf.shape[1] // 2
+    x_copies = []
+    for h in range(2):
+        rows = pl.ds(h * half, half)
+        for i, off in ((1, 1), (2, 3)):
+            hh = h if i == 1 else 1 - h
+            rows = pl.ds(hh * half, half)
+            cp = remote(xbuf.at[0, rows], xbuf.at[i, rows], sa_x.at[i, hh], ra_x.at[i, hh], first_dev(off))
+            cp.start()
+            x_copies.append(cp)
+    r_copies = []
+    for i, off in ((1, 1), (2, 3), (3, 2)):
+        cp = remote(rbuf.at[0], rbuf.at[i], sa_r.at[i], ra_r.at[i], first_dev(off))
+        cp.start()
+        r_copies.append(cp)
+
+    tokens = xbuf.shape[1]
+    row_i = lax.broadcasted_iota(jnp.int32, (tokens, tokens), 0)
+    col_i = lax.broadcasted_iota(jnp.int32, (tokens, tokens), 1)
+    before = jnp.where(row_i < col_i, 1.0, 0.0).astype(jnp.bfloat16)
+    experts = router_ref.shape[0]
+    width = xbuf.shape[2]
+
+    def make_tables(i):
+        r = rbuf[i]
+        ei = lax.broadcasted_iota(jnp.int32, (experts, tokens), 0)
+        hit = ei == r[0:1, :]
+        for k in range(1, TOPK):
+            hit = jnp.logical_or(hit, ei == r[k:k + 1, :])
+        hit_f = jnp.where(hit, 1.0, 0.0)
+        rank = jnp.dot(hit_f.astype(jnp.bfloat16), before, preferred_element_type=jnp.float32)
+        rank_s[i] = jnp.where(hit, rank, -1.0)
+        logits = lax.dot_general(router_ref[...], xbuf[i], (((1,), (1,)), ((), ())),
+                                 preferred_element_type=jnp.float32)
+        sig = jnp.where(hit, jax.nn.sigmoid(logits), 0.0)
+        gate_s[i] = sig / jnp.sum(sig, axis=0, keepdims=True)
+
+    slot_i = lax.broadcasted_iota(jnp.int32, (CAP, tokens), 0).astype(jnp.float32)
+    tile = 512
+
+    def dispatch(i):
+        picks = []
+        for j in range(4):
+            for dc in range(2):
+                e = second_exp(j, dc)
+                rank_row = rank_s[i, pl.ds(e, 1), :]
+                gate_row = gate_s[i, pl.ds(e, 1), :]
+                eq = slot_i == rank_row
+                picks.append(jnp.where(eq, 1.0, 0.0).astype(jnp.bfloat16))
+                q = j * 2 + dc
+                ct_s[i, q * CAP:(q + 1) * CAP, :] = jnp.where(eq, gate_row, 0.0).astype(jnp.bfloat16)
+        pick = jnp.concatenate(picks, axis=0)
+
+        @pl.loop(0, width // tile)
+        def _(n):
+            cols = pl.ds(pl.multiple_of(n * tile, tile), tile)
+            rows = jnp.dot(pick, xbuf[i, :, cols], preferred_element_type=jnp.float32).astype(jnp.bfloat16)
+            arrived[i, 0:CAP, cols] = rows[0:CAP]
+            pack[i, :, cols] = rows
+        for q in range(1, 8):
+            pack_copy(i, q).start()
+
+    def pack_copy(i, q):
+        j, dc = q // 2, q % 2
+        return remote(pack.at[i, pl.ds(q * CAP, CAP)], arrived.at[i, pl.ds(q * CAP, CAP)],
+                      sb_p.at[i, q], rb_p.at[i, q], (x, second_exp(j, dc)))
+
+    def result_copy(i, q):
+        j, dc = q // 2, q % 2
+        return remote(result.at[i, pl.ds(q * CAP, CAP)], returned.at[i, pl.ds(q * CAP, CAP)],
+                      sb_r.at[i, q], rb_r.at[i, q], relay_dev(j, dc))
+
+    def expert(i):
+        for q in range(1, 8):
+            pack_copy(i, q).wait_recv()
+
+        @pl.loop(0, FFE // 256)
+        def _(n):
+            up_cols = pl.ds(pl.multiple_of(FFE + n * 256, 256), 256)
+            cols = pl.ds(pl.multiple_of(n * 256, 256), 256)
+            a = arrived[i]
+            g = jnp.dot(a, wgu_ref[:, cols], preferred_element_type=jnp.float32)
+            u = jnp.dot(a, wgu_ref[:, up_cols], preferred_element_type=jnp.float32)
+            units[:, cols] = (jnp.maximum(g, 0.0) * u).astype(jnp.bfloat16)
+
+        @pl.loop(0, width // tile)
+        def _(n):
+            cols = pl.ds(pl.multiple_of(n * tile, tile), tile)
+            rows = jnp.dot(units[...], wdn_ref[:, cols], preferred_element_type=jnp.float32).astype(jnp.bfloat16)
+            returned[i, 0:CAP, cols] = rows[0:CAP]
+            result[i, :, cols] = rows
+        for q in range(1, 8):
+            result_copy(i, q).start()
+
+    offsets = (0, 1, 3, 2)
+
+    def partial_copy(i):
+        return remote(psend.at[i - 1], precv.at[i - 1], sp_s.at[i - 1], sp_r.at[i - 1],
+                      first_dev(4 - offsets[i]))
+
+    def combine(i):
+        for q in range(1, 8):
+            result_copy(i, q).wait_recv()
+
+        @pl.loop(0, width // tile)
+        def _(n):
+            cols = pl.ds(pl.multiple_of(n * tile, tile), tile)
+            part = lax.dot_general(ct_s[i], returned[i, :, cols], (((0,), (0,)), ((), ())),
+                                   preferred_element_type=jnp.float32)
+            if i == 0:
+                acc[:, cols] = acc[:, cols] + part
+            else:
+                psend[i - 1, :, cols] = part.astype(jnp.bfloat16)
+        if i:
+            partial_copy(i).start()
+
+    def forward(i):
+        h = 0 if i == 1 else 1
+        rows = pl.ds(h * half, half)
+        return remote(xbuf.at[i, rows], xbuf.at[3, rows], sa_x.at[3, h], ra_x.at[3, h],
+                      first_dev(1 if i == 1 else 3))
+
+    make_tables(0)
+    dispatch(0)
+    x_copies[0].wait_recv()
+    forward(1).start()
+    x_copies[1].wait_recv()
+    forward(2).start()
+    for i in (1, 2, 3):
+        r_copies[i - 1].wait_recv()
+        if i == 3:
+            forward(1).wait_recv()
+            forward(2).wait_recv()
+        else:
+            x_copies[2 + i - 1].wait_recv()
+        make_tables(i)
+        dispatch(i)
+        expert(i - 1)
+        if i >= 2:
+            combine(i - 2)
+    expert(3)
+    combine(2)
+    combine(3)
+    for i in (1, 2, 3):
+        partial_copy(i).wait_recv()
+    out_ref[...] = (acc[...] + precv[0].astype(jnp.float32) + precv[1].astype(jnp.float32)
+                    + precv[2].astype(jnp.float32)).astype(jnp.bfloat16)
+    for cp in x_copies + r_copies:
+        cp.wait_send()
+    forward(1).wait_send()
+    forward(2).wait_send()
+    for i in range(4):
+        for q in range(1, 8):
+            pack_copy(i, q).wait_send()
+            result_copy(i, q).wait_send()
+        if i:
+            partial_copy(i).wait_send()
+
+
+def moe(hidden, expert_norm_gain, routes, router, expert_gate_up, expert_down):
+    tokens, width = hidden.shape
+    experts = router.shape[1]
+    routes_t = jnp.concatenate(
+        [routes.T, jnp.full((8 - TOPK, tokens), -1, jnp.int32)], axis=0)
+    bf, f32 = jnp.bfloat16, jnp.float32
+    rows = 8 * CAP
+    dma = pltpu.SemaphoreType.DMA
+    return pl.pallas_call(
+        moe_kernel,
+        out_shape=jax.ShapeDtypeStruct((tokens, width), bf),
+        in_specs=[pl.BlockSpec(memory_space=pltpu.VMEM)] * 6,
+        out_specs=pl.BlockSpec(memory_space=pltpu.VMEM),
+        scratch_shapes=[
+            pltpu.VMEM((4, tokens, width), bf),
+            pltpu.VMEM((4, 8, tokens), jnp.int32),
+            pltpu.VMEM((4, experts, tokens), f32),
+            pltpu.VMEM((4, experts, tokens), f32),
+            pltpu.VMEM((4, rows, tokens), bf),
+            pltpu.VMEM((4, rows, width), bf),
+            pltpu.VMEM((4, rows, width), bf),
+            pltpu.VMEM((rows, FFE), bf),
+            pltpu.VMEM((4, rows, width), bf),
+            pltpu.VMEM((4, rows, width), bf),
+            pltpu.VMEM((3, tokens, width), bf),
+            pltpu.VMEM((3, tokens, width), bf),
+            pltpu.VMEM((tokens, width), f32),
+            dma((4, 2)), dma((4, 2)), dma((4,)), dma((4,)),
+            dma((4, 8)), dma((4, 8)), dma((4, 8)), dma((4, 8)),
+            dma((3,)), dma((3,)),
+        ],
+        compiler_params=pltpu.CompilerParams(
+            collective_id=1, has_side_effects=True, vmem_limit_bytes=60 * 1024 * 1024),
+        name="moe",
+    )(hidden, expert_norm_gain.reshape(1, width), routes_t, router.T,
+      expert_gate_up.reshape(expert_gate_up.shape[-2:]), expert_down.reshape(expert_down.shape[-2:]))
 
 
 def on_device(
@@ -227,39 +468,7 @@
         adapter_output_down,
         adapter_output_up,
     )
-    ffn_normed = rms_norm(hidden_state, expert_norm_gain)
-    gates = gate_weights(ffn_normed, router, routes)
-    local_experts = expert_gate_up.shape[0]
-    experts = local_experts * lax.axis_size("exp")
-    capacity = 3 * new_token_count * TOPK // (2 * experts)
-    destination = slot_of(routes, experts, capacity)
-    slot_total = experts * capacity
-    matches = jnp.arange(slot_total, dtype=jnp.int32)[:, None] == destination[None, :]
-    source = jnp.arange(new_token_count * TOPK, dtype=jnp.int32) // TOPK
-    source_tok = jnp.sum(jnp.where(matches, source[None, :], 0), axis=1)
-    filled = jnp.any(matches, axis=1)
-    outgoing = jnp.where(
-        filled[:, None], jnp.take(ffn_normed, source_tok, axis=0), jnp.zeros((), jnp.bfloat16)
-    )
-    outgoing = outgoing.reshape(experts, capacity, -1)
-    arrived = lax.all_to_all(outgoing, "exp", split_axis=0, concat_axis=0, tiled=True)
-    sources = arrived.shape[0] // local_experts
-    item_count = arrived.shape[1]
-    arranged = arrived.reshape(sources, local_experts, item_count, -1)
-    inner = jnp.einsum(
-        "sxcd,xdf->sxcf", arranged, expert_gate_up, preferred_element_type=jnp.float32
-    )
-    half_width = inner.shape[-1] // 2
-    units = (jax.nn.relu(inner[..., :half_width]) * inner[..., half_width:]).astype(jnp.bfloat16)
-    result = jnp.einsum(
-        "sxcf,xfd->sxcd", units, expert_down, preferred_element_type=jnp.float32
-    ).astype(jnp.bfloat16)
-    result = result.reshape(sources * local_experts, item_count, -1)
-    returned = lax.all_to_all(result, "exp", split_axis=0, concat_axis=0, tiled=True)
-    picked = jnp.take(returned.reshape(slot_total, -1), destination, axis=0).astype(jnp.float32)
-    picked = picked.reshape(new_token_count, TOPK, -1)
-    mixed_rows = hidden_state.astype(jnp.float32) + jnp.sum(gates[..., None] * picked, axis=1)
-    return mixed_rows.astype(jnp.bfloat16)
+    return moe(hidden_state, expert_norm_gain, routes, router, expert_gate_up, expert_down)
 
 
 def solution(mesh):

time: 312 us -> 217 us (0.70); the launches traced: 307 us -> 216 us
  Pallas kernels: 0 us -> 94.6 us
  blocking collectives: 61.1 us -> 0 us
  local copies, waits for them, and re-layouts: 58.8 us -> 22.1 us
  other arithmetic: 50.3 us -> 13.9 us
  waiting for transfers between devices: 67.4 us -> 42.6 us
  matrix products: 50.9 us -> 29.2 us
  starting transfers between devices: 4.77 us -> 0.01 us
    pallas_call x0 -> x1, Pallas kernels: none -> 94.6 us  [moe(): pl.pallas_call(moe_kernel, out_shape=jax.ShapeDtypeStruct((tokens, width)...]
    all_to_all x1 -> x0, blocking collectives: 61.1 us -> none  [on_device(): lax.all_to_all(outgoing, 'exp', split_axis=0, concat_axis=0, tiled=True)]
    all_to_all x1 -> x0, waiting for transfers between devices: 47.7 us -> none  [on_device(): lax.all_to_all(result, 'exp', split_axis=0, concat_axis=0, tiled=True)]
    gather x8 -> x0, local copies, waits for them, and re-layouts: 31.7 us -> none  [the longest x2 16.3 us: on_device(): jnp.take(returned.reshape(slot_total, -1), destination, axis=0)]
    all_gather x1, waiting for transfers between devices: 19 us -> 41.9 us  [on_device(): lax.all_gather(shared_prompt_cache, ('req', 'exp'), axis=0, tiled=True)]
    reduce_sum x4 -> x0, other arithmetic: 17 us -> none  [the longest x1 16.2 us: on_device(): jnp.sum(gates[..., None] * picked, axis=1)]
    dot_general x3 -> x0, matrix products: 15.5 us -> none  [the longest x1 9.72 us: on_device(): jnp.einsum('sxcd,xdf->sxcf', arranged, expert_gate_up, preferred_element_...]
    another operation x5 -> x2, other arithmetic: 12.5 us -> 2.96 us
  transfers between devices with their start and end apart: 2 -> 1, of which waited for: 2 -> 1; matrix products, arithmetic and copies ran while one was open for 22% -> 16% of each run, Pallas kernels for 0% -> 0%
where the time goes in v1:
time: 217 us; the launch traced here: 216 us
  Pallas kernels  94.6 us (44%)
  waiting for transfers between devices  42.6 us (20%)
  matrix products  29.2 us (13%)
  local copies, waits for them, and re-layouts  22.1 us (10%)
  other arithmetic  13.9 us (6%)
  between operations  13.7 us (6%)
    pallas_call x1, Pallas kernels, moe(): pl.pallas_call(moe_kernel, out_shape=jax.ShapeDtypeStruct((tokens, width)...  94.6 us
    all_gather x1, waiting for transfers between devices, on_device(): lax.all_gather(shared_prompt_cache, ('req', 'exp'), axis=0, tiled=True)  41.9 us
    dot_general x2, matrix products, adapter_update(): return jnp.dot(inner, up_proj, preferred_element_type=jnp.float32)  8.01 us
    gather x2, local copies, waits for them, and re-layouts, on_device(): jnp.take(complete_cache, requested_pages, axis=0)  7.1 us
    dot_general x2, matrix products, block_attention(): jnp.einsum('tkgd,nkd->tkgn', grouped_queries, key_matrix, preferred_eleme...  5.31 us
    dot_general x1, matrix products, finalize(): jnp.dot(attention_output, attention_output_weight, preferred_element_type...  5.03 us
    dot_general x1, matrix products, apply_projection(): jnp.dot(normalized, query_matrix, preferred_element_type=jnp.float32)  5 us
  transfers between devices with their start and end apart: 1, of which 1 were waited for; matrix products, arithmetic and copies ran while one was open for 16% of the time, Pallas kernels for 0%

profile of v1, /device:TPU:1, one launch (start us, length us, event | category | flops | bytes accessed | tf_op | source)
XLA Modules:
  0.0 216.2 jit_solution(6791642231995648621)
XLA Ops:
  10.7 1.3 reshape.271.gain_ref
  16.3 1.4 fusion.11
  17.7 1.7 fusion.59
  20.6 5.0 %fusion.57 = f32[256,1536]{1,0:T(8,128)} fusion(bf16[1536,1536]{1,0:T(8,128)(2,1)} %param.27, bf16[256,1536]{1,0:T(8,128)(2,1)S(1)} %copy-done.2, f32[1536]{0:T(1024)S(1)} %convert_element_type.52, f32[256]{0:T(256)S(1)} %add_rsqrt_fusion), kind=kOutput, calls=%fused_computation.105 | convolution fusion | flops 1209532416 | bytes 7085056 | tf_op jit(solution)/shard_map/dot_general | solution.py:80
  25.6 4.2 %convolution_add_fusion.1 = f32[256,1536]{1,0:T(8,128)} fusion(f32[256,1536]{1,0:T(8,128)} %fusion.57, bf16[256,1536]{1,0:T(8,128)(2,1)} %param.31, bf16[1536,256]{1,0:T(8,128)(2,1)} %param.30, s32[256]{0:T(256)S(1)} %and_select_fusion, s32[256]{0:T(256)S(1)} %get-tuple-element.5, bf16[256,1536]{1,0:T(8,128)(2,1)S(1)} %copy-done.2, ...), kind=kOutput, calls=%fused_computation.13 | convolution fusion | flops 404815872 | bytes 5514240 | tf_op jit(solution)/shard_map/dot_general | solution.py:52
  29.7 1.9 copy.68
  31.6 1.9 subtract_convert_fusion
  33.9 1.4 copy.70
  36.9 1.5 fusion.61
  38.4 1.0 subtract_convert_fusion.1
  39.5 2.8 %fusion.10 = (f32[256,2,6]{0,2,1:T(8,128)S(1)}, f32[2,256,256,6]{2,1,3,0:T(8,128)}) fusion(pred[256,256]{0,1:T(8,128)(4,1)S(1)} %fusion.30, bf16[256,2,6,64]{3,0,2,1:T(8,128)(2,1)S(1)} %bitcast.78, bf16[256,2,6,64]{3,0,2,1:T(8,128)(2,1)S(1)} %bitcast.76, bf16[256,2,64]{2,0,1:T(8,128)(2,1)S(1)} %get-tuple-element.12, ...), kind=kOutput, calls=%fused_computation.17 | convolution fusion | flops 205517824 | bytes 4141056 | tf_op jit(solution)/shard_map/tkgd,nkd->tkgn/dot_general | solution.py:118
  42.2 41.9 %all-gather.2.cloned.1.call-done = bf16[512,16,512]{2,1,0:T(8,128)(2,1)} async-done(((bf16[4,16,512]{2,1,0:T(8,128)(2,1)}), bf16[512,16,512]{2,1,0:T(8,128)(2,1)}) %all-gather.2.cloned.1.call-update) | async-done | bytes 8388624 | tf_op jit(solution)/shard_map/all_gather | solution.py:444
  84.1 5.0 %gather_fusion.1 = bf16[64,16,512]{2,1,0:T(8,128)(2,1)} fusion(bf16[512,16,512]{2,1,0:T(8,128)(2,1)} %all-gather.2.cloned.1.call-done, s32[1024]{0:T(1024)S(1)} %pad_clamp_fusion), kind=kCustom, calls=%fused_computation.1 | custom fusion | bytes 2097408 | tf_op jit(solution)/shard_map/jit(_take)/gather | solution.py:445
  89.1 2.1 gather.12
  91.2 1.4 copy_select_fusion
  92.7 2.5 %fusion.2 = (f32[256,2,6]{0,2,1:T(8,128)S(1)}, f32[2,1024,256,6]{2,1,3,0:T(8,128)S(1)}) fusion(pred[256,1024]{0,1:T(8,128)(4,1)S(1)} %broadcast_compare_fusion, bf16[256,2,6,64]{3,0,2,1:T(8,128)(2,1)S(1)} %bitcast.79, bf16[256,2,6,64]{3,0,2,1:T(8,128)(2,1)S(1)} %bitcast.77, bf16[1024,4,128]{2,0,1:T(8,128)(2,1)S(1)} %copy_select_fusion), kind=kOutput, calls=%fused_computation.6 | convolution fusion | flops 816313344 | bytes 14954496 | tf_op jit(solution)/shard_map/tkgd,nkd->tkgn/dot_general | solution.py:118
  96.1 0.9 fusion.14
  97.1 2.5 %fusion = f32[256,2,6]{0,2,1:T(8,128)S(1)} fusion(f32[2,1024,256,6]{2,1,3,0:T(8,128)S(1)} %get-tuple-element.23, f32[256,2,6]{0,2,1:T(8,128)S(1)} %get-tuple-element.16, pred[256,1024]{0,1:T(8,128)(4,1)S(1)} %broadcast_compare_fusion), kind=kLoop, calls=%fused_computation.4 | loop fusion | flops 12579840 | bytes 12869632 | tf_op jit(solution)/shard_map/reduce_sum | solution.py:127
  99.6 3.2 %fusion.17 = bf16[256,2,6,128]{0,3,2,1:T(8,128)(2,1)S(1)} fusion(f32[2,128,256,6]{2,1,3,0:T(8,128)S(1)} %fusion.14, f32[2,1024,256,6]{2,1,3,0:T(8,128)S(1)} %get-tuple-element.23, f32[256,2,6]{0,2,1:T(8,128)S(1)} %get-tuple-element.16, pred[256,1024]{0,1:T(8,128)(4,1)S(1)} %broadcast_compare_fusion, f32[256,2,6]{0,2,1:T(8,128)S(1)} %get-tuple-element.7, ...), kind=kOutput, calls=%fused_computation.26 | convolution fusion | flops 819855360 | bytes 15794176 | tf_op jit(solution)/shard_map/tkgn,nkd->tkgd/dot_general | solution.py:128
  102.9 0.9 copy-done.6
  103.8 5.0 %fusion.62 = f32[256,1536]{1,0:T(8,128)} fusion(bf16[256,1536]{0,1:T(8,128)(2,1)S(1)} %bitcast.83, bf16[1536,1536]{1,0:T(8,128)(2,1)} %param.29), kind=kOutput, calls=%fused_computation.108 | convolution fusion | flops 1207959552 | bytes 7077888 | tf_op jit(solution)/shard_map/dot_general | solution.py:105
  108.8 3.8 %fusion.9.hid_ref = bf16[256,1536]{1,0:T(8,128)(2,1)} fusion(f32[256,1536]{1,0:T(8,128)} %fusion.62, bf16[256,1536]{1,0:T(8,128)(2,1)S(1)} %copy-done.5, bf16[256,1536]{1,0:T(8,128)(2,1)S(1)} %copy-done.3, bf16[256,1536]{0,1:T(8,128)(2,1)} %bitcast.84, bf16[1536,256]{1,0:T(8,128)(2,1)} %param.32, s32[256]{0:T(256)S(1)} %copy-done.13, ...), kind=kOutput, calls=%fused_computation.16 | convolution fusion | flops 404422656 | bytes 5507072 | tf_op jit(solution)/shard_map/dot_general | solution.py:52
  112.6 94.6 %moe.1 = bf16[256,1536]{1,0:T(8,128)(2,1)} custom-call(bf16[256,1536]{1,0:T(8,128)(2,1)} %fusion.9.hid_ref, bf16[1,1536]{1,0:T(2,128)(2,1)} %reshape.271.gain_ref, s32[8,256]{1,0:T(8,128)} %concatenate.20.routes_ref, bf16[32,1536]{1,0:T(8,128)(2,1)} %bitcast.85, bf16[1536,1536]{1,0:T(8,128)(2,1)} %bitcast.81, bf16[768,1536]{1,0:T(8,128)(2,1)} %bitcast.82), custom_call_target="tpu_custom_call" | custom-call | tf_op jit(solution)/shard_map/moe/pallas_call | solution.py:360
  207.3 2.1 copy.93
  (63 shorter events, 12.4 us)
Async XLA Ops:
  6.5 11.1 %copy-start = (bf16[1536,512]{1,0:T(8,128)(2,1)S(1)}, bf16[1536,512]{1,0:T(8,128)(2,1)}, u32[]{:S(2)}) copy-start(bf16[1536,512]{1,0:T(8,128)(2,1)} %param.28) | copy-start | bytes 4718596
  6.5 77.6 %all-gather.2.cloned.1.call-start = ((), (), s32[]{:S(2)}) async-start(), calls=%async_computation | async-start | bytes 8454144 | tf_op jit(solution)/shard_map/all_gather | solution.py:444
  14.4 6.1 %copy-start.2 = (bf16[256,1536]{1,0:T(8,128)(2,1)S(1)}, bf16[256,1536]{1,0:T(8,128)(2,1)}, u32[]{:S(2)}) copy-start(bf16[256,1536]{1,0:T(8,128)(2,1)} %param.19) | copy-start | bytes 2359300
  14.7 2.9 %copy-start.7 = (f32[256,64]{0,1:T(8,128)}, f32[256,64]{0,1:T(8,128)S(1)}, u32[]{:S(2)}) copy-start(f32[256,64]{0,1:T(8,128)S(1)} %get-tuple-element.18) | copy-start | bytes 196612
  14.7 2.9 %copy-start.8 = (f32[256,64]{0,1:T(8,128)}, f32[256,64]{0,1:T(8,128)S(1)}, u32[]{:S(2)}) copy-start(f32[256,64]{0,1:T(8,128)S(1)} %get-tuple-element.19) | copy-start | bytes 196612
  19.6 5.9 %copy-start.4 = (f32[256,4,128]{2,1,0:T(4,128)}, f32[256,4,128]{2,1,0:T(4,128)S(1)}, u32[]{:S(2)}) copy-start(f32[256,4,128]{2,1,0:T(4,128)S(1)} %reshape.268) | copy-start | bytes 1572868
  20.5 5.0 %copy-start.12 = (s32[256]{0:T(256)}, s32[256]{0:T(256)S(1)}, u32[]{:S(2)}) copy-start(s32[256]{0:T(256)S(1)} %and_select_fusion) | copy-start | bytes 3076
  31.6 3.7 %copy-start.11 = (s32[256,4]{0,1:T(4,128)S(1)}, s32[256,4]{0,1:T(4,128)}, u32[]{:S(2)}) copy-start(s32[256,4]{0,1:T(4,128)} %param.25) | copy-start | bytes 12292
  31.6 4.9 %copy-start.10 = (s32[1,256]{1,0:T(1,128)S(1)}, s32[1,256]{1,0:T(1,128)}, u32[]{:S(2)}) copy-start(s32[1,256]{1,0:T(1,128)} %param.20) | copy-start | bytes 3076
  92.7 2.6 %copy-start.1 = (f32[2,256,256,6]{2,1,3,0:T(8,128)S(1)}, f32[2,256,256,6]{2,1,3,0:T(8,128)}, u32[]{:S(2)}) copy-start(f32[2,256,256,6]{2,1,3,0:T(8,128)} %get-tuple-element.21) | copy-start | bytes 9437188
  95.2 0.9 copy-start.9
  102.9 0.9 copy-start.6
  103.8 5.0 %copy-start.3 = (bf16[256,1536]{1,0:T(8,128)(2,1)S(1)}, bf16[256,1536]{1,0:T(8,128)(2,1)}, u32[]{:S(2)}) copy-start(bf16[256,1536]{1,0:T(8,128)(2,1)} %param.19) | copy-start | bytes 2359300
  103.8 5.0 %copy-start.5 = (bf16[256,1536]{1,0:T(8,128)(2,1)S(1)}, bf16[256,1536]{1,0:T(8,128)(2,1)}, u32[]{:S(2)}) copy-start(bf16[256,1536]{1,0:T(8,128)(2,1)} %param.33) | copy-start | bytes 2359300
  103.8 5.0 %copy-start.13 = (s32[256]{0:T(256)S(1)}, s32[256]{0:T(256)}, u32[]{:S(2)}) copy-start(s32[256]{0:T(256)} %copy-done.12) | copy-start | bytes 3076
Sparse Core Ops, SparseCore 0:
  10.3 73.7 all-gather.1

commit v2 on v1

--- a/solution.py
+++ b/solution.py
@@ -1,3 +1,5 @@
+import math
+
 import jax
 import jax.numpy as jnp
 from jax import lax
@@ -23,116 +25,334 @@
 VERY_NEGATIVE = -1e30
 
 
-def rms_norm(weight_matrix, gain_vector):
-    values = weight_matrix.astype(jnp.float32)
-    factor = lax.rsqrt(jnp.mean(values * values, axis=-1, keepdims=True) + EPSILON)
-    return (values * factor * gain_vector.astype(jnp.float32)).astype(jnp.bfloat16)
-
-
-def apply_rotary(values, token_positions):
-    half_width = values.shape[-1] // 2
-    frequency = THETA ** (-jnp.arange(half_width).astype(jnp.float32) / half_width)
-    angles = token_positions.astype(jnp.float32)[:, None] * frequency[None, :]
-    cosine = jnp.cos(angles)[:, None, :]
-    sine_table = jnp.sin(angles)[:, None, :]
-    first_half = values[..., :half_width]
-    second = values[..., half_width:]
-    return jnp.concatenate(
-        [first_half * cosine - second * sine_table, second * cosine + first_half * sine_table],
-        axis=-1,
-    )
-
-
-def adapter_update(weight_matrix, down_proj, up_proj, token_adapter):
-    inner = jnp.dot(weight_matrix, down_proj, preferred_element_type=jnp.float32)
-    owner_slot = jnp.arange(down_proj.shape[1], dtype=jnp.int32) // ADAPTER_RANK
-    inner = jnp.where(owner_slot[None, :] == token_adapter[:, None], inner, 0.0).astype(
-        jnp.bfloat16
-    )
-    return jnp.dot(inner, up_proj, preferred_element_type=jnp.float32)
-
-
-def request_info(request_row, prompt_req, adapter_req):
-    new_token_count = request_row.shape[0]
-    request_slot_count = prompt_req.shape[0]
-    matches = request_row[:, None] == jnp.arange(request_slot_count, dtype=jnp.int32)[None, :]
-    token_adapter = jnp.sum(jnp.where(matches, adapter_req[None, :], 0), axis=1)
-    prompt_tok = jnp.sum(jnp.where(matches, prompt_req[None, :], 0), axis=1)
-    token_index = jnp.arange(new_token_count, dtype=jnp.int32)
-    first_row = jnp.min(jnp.where(matches, token_index[:, None], new_token_count), axis=0)
-    start_tok = jnp.sum(jnp.where(matches, first_row[None, :], 0), axis=1)
-    token_positions = PROMPT_LENGTH + token_index - start_tok
-    return (token_adapter, prompt_tok, token_positions)
-
-
-def apply_projection(
-    tokens,
-    token_adapter,
-    token_positions,
-    attention_norm_gain,
-    query_matrix,
-    key_value_weight,
-    adapter_query_down,
-    adapter_query_up,
+TILE_GROUPS = ((0, 6), (6, 5), (11, 5))
+AXIS_ORDERS = ((0, 1, 2), (1, 2, 0), (2, 0, 1))
+
+
+def front_kernel(
+    slot_ref, prompt_ref, adapter_ref, table_ref, tokens_ref, cache_ref, gain_ref,
+    wq_any, wkv_any, aqd_any, aqu_any, wo_any, aod_any, aou_any,
+    hid_ref,
+    cache, wq, wkv, aqd, aqu, wo, aod, aou,
+    normed, inner_s, cos_s, sin_s, q_s, k_s, v_s, kv_s, att,
+    w_sem, c_sem, ag_s, ag_r, co_s, co_r,
 ):
-    new_token_count = tokens.shape[0]
-    normalized = rms_norm(tokens, attention_norm_gain)
-    query_rows = jnp.dot(normalized, query_matrix, preferred_element_type=jnp.float32)
-    query_rows = query_rows + adapter_update(
-        normalized, adapter_query_down, adapter_query_up, token_adapter
-    )
-    query_rows = apply_rotary(
-        query_rows.reshape(new_token_count, QUERY_HEADS, HEAD_WIDTH), token_positions
-    ).astype(jnp.bfloat16)
-    key_value_rows = jnp.dot(
-        normalized, key_value_weight, preferred_element_type=jnp.float32
-    ).reshape(new_token_count, 2 * KEY_VALUE_HEADS, HEAD_WIDTH)
-    key_matrix = apply_rotary(key_value_rows[:, :KEY_VALUE_HEADS], token_positions).astype(
-        jnp.bfloat16
-    )
-    value_matrix = key_value_rows[:, KEY_VALUE_HEADS:].astype(jnp.bfloat16)
-    return (query_rows, key_matrix, value_matrix)
-
-
-def finalize(
-    attention_output,
-    tokens,
-    token_adapter,
-    attention_output_weight,
-    adapter_output_down,
-    adapter_output_up,
-):
-    expert_mixture = jnp.dot(
-        attention_output, attention_output_weight, preferred_element_type=jnp.float32
-    )
-    expert_mixture = expert_mixture + adapter_update(
-        attention_output, adapter_output_down, adapter_output_up, token_adapter
-    )
-    return (tokens.astype(jnp.float32) + expert_mixture).astype(jnp.bfloat16)
-
-
-def block_attention(running, grouped_queries, key_matrix, value_matrix, allowed):
-    running_max, totals, accum = running
-    scale = grouped_queries.shape[-1] ** (-0.5)
-    scores = (
-        jnp.einsum(
-            "tkgd,nkd->tkgn", grouped_queries, key_matrix, preferred_element_type=jnp.float32
-        )
-        * scale
-    )
-    scores = jnp.where(allowed[:, None, None, :], scores, VERY_NEGATIVE)
-    new_max = jnp.maximum(running_max, jnp.max(scores, axis=-1))
-    factor = jnp.exp(running_max - new_max)
-    weights = jnp.exp(scores - new_max[..., None])
-    totals = totals * factor + jnp.sum(weights, axis=-1)
-    summed = jnp.einsum(
-        "tkgn,nkd->tkgd",
-        weights.astype(jnp.bfloat16),
-        value_matrix,
-        preferred_element_type=jnp.float32,
-    )
-    accum = accum * factor[..., None] + summed
-    return (new_max, totals, accum)
+    x = lax.axis_index("req")
+    e_me = lax.axis_index("exp")
+    y = e_me // 8
+    z = lax.rem(e_me // 2, 4)
+    c = lax.rem(e_me, 2)
+    here = (x, y, z)
+
+    def device(axis, offset):
+        p = list(here)
+        p[axis] = lax.rem(p[axis] + offset, 4)
+        return (p[0], (p[1] * 4 + p[2]) * 2 + c)
+
+    partner = (x, (y * 4 + z) * 2 + 1 - c)
+
+    barrier = pltpu.get_barrier_semaphore()
+    for axis in range(3):
+        for off in (1, 3):
+            pl.semaphore_signal(barrier, 1, device_id=device(axis, off), device_id_type=MESH)
+    pl.semaphore_signal(barrier, 1, device_id=partner, device_id_type=MESH)
+
+    own = []
+    for p in range(4):
+        for col in range(4):
+            cp = pltpu.make_async_copy(
+                cache_ref.at[p, :, pl.ds(col * 128, 128)],
+                cache.at[x, y, z, c, p * 4 + col], c_sem.at[p * 4 + col])
+            cp.start()
+            own.append(cp)
+    weights = []
+    for i, (src, dst) in enumerate((
+            (wkv_any, wkv), (aqd_any, aqd), (aqu_any, aqu), (wq_any, wq),
+            (aod_any, aod), (wo_any, wo), (aou_any, aou))):
+        cp = pltpu.make_async_copy(src, dst, w_sem.at[i])
+        cp.start()
+        weights.append(cp)
+
+    def block(where, first, count):
+        return cache.at[where[0], where[1], where[2], c, pl.ds(first, count)]
+
+    def step(g, phase, kind, axis, where):
+        lo, n = TILE_GROUPS[g]
+        if kind == 2:
+            n = n // 2
+        elif kind == 3:
+            lo, n = lo + n // 2, n - n // 2
+        view = block(where, lo, n)
+        return pltpu.make_async_remote_copy(
+            src_ref=view, dst_ref=view, send_sem=ag_s.at[g, phase, kind], recv_sem=ag_r.at[g, phase, kind],
+            device_id=device(axis, 1 if kind in (0, 2) else 3), device_id_type=MESH)
+
+    every = slice(None)
+
+    def place(g, second, third):
+        order = AXIS_ORDERS[g]
+        w = [every, every, every]
+        for axis, off in ((order[1], second), (order[2], third)):
+            if off is not None:
+                w[axis] = lax.rem(here[axis] + off, 4)
+        return w
+
+    class Ring:
+        def __init__(self, g, phase, axis, where_of):
+            self.g, self.phase, self.axis, self.where_of = g, phase, axis, where_of
+
+        def cp(self, kind, off):
+            return step(self.g, self.phase, kind, self.axis, self.where_of(off))
+
+        def begin(self):
+            self.cp(0, 0).start()
+            self.cp(1, 0).start()
+
+        def pass_on(self):
+            self.cp(0, 3).wait_recv()
+            self.cp(2, 3).start()
+            self.cp(1, 1).wait_recv()
+            self.cp(3, 1).start()
+
+        def finish(self):
+            self.cp(2, 2).wait_recv()
+            self.cp(3, 2).wait_recv()
+
+        def drain(self):
+            self.cp(0, 0).wait_send()
+            self.cp(1, 0).wait_send()
+            self.cp(2, 3).wait_send()
+            self.cp(3, 1).wait_send()
+
+    def first_where(g):
+        def f(off):
+            order = AXIS_ORDERS[g]
+            w = [here[0], here[1], here[2]]
+            w[order[0]] = lax.rem(here[order[0]] + off, 4)
+            return w
+        return f
+
+    groups = range(3)
+    ring1 = [Ring(g, 0, AXIS_ORDERS[g][0], first_where(g)) for g in groups]
+    ring2 = [Ring(g, 1, AXIS_ORDERS[g][1], lambda off, g=g: place(g, off, 0)) for g in groups]
+    ring3 = [[Ring(g, 2 + o, AXIS_ORDERS[g][2], lambda off, g=g, o=o: place(g, o, off)) for o in range(4)]
+             for g in groups]
+
+    def share(g, i, second, third):
+        lo, n = TILE_GROUPS[g]
+        view = block(place(g, second, third), lo, n)
+        return pltpu.make_async_remote_copy(
+            src_ref=view, dst_ref=view, send_sem=co_s.at[g, i], recv_sem=co_r.at[g, i],
+            device_id=partner, device_id_type=MESH)
+
+    def share_mine(g, i):
+        if i == 0:
+            return share(g, 0, None, 0)
+        return share(g, i, (i - 1) // 3, 1 + (i - 1) % 3)
+
+    def theirs(g, i):
+        lo, n = TILE_GROUPS[g]
+        second, third = (None, 0) if i == 0 else ((i - 1) // 3, 1 + (i - 1) % 3)
+        w = place(g, second, third)
+        view = cache.at[w[0], w[1], w[2], 1 - c, pl.ds(lo, n)]
+        return pltpu.make_async_remote_copy(
+            src_ref=view, dst_ref=view, send_sem=co_s.at[g, i], recv_sem=co_r.at[g, i],
+            device_id=partner, device_id_type=MESH)
+
+    tokens = tokens_ref.shape[0]
+    width = tokens_ref.shape[1]
+    half_rows = tokens // 2
+
+    for cp in own:
+        cp.wait()
+    pl.semaphore_wait(barrier, 7)
+    for g in groups:
+        ring1[g].begin()
+
+    tv = tokens_ref[...].astype(jnp.float32)
+    factor = lax.rsqrt(jnp.mean(tv * tv, axis=-1, keepdims=True) + EPSILON)
+    normed[...] = (tv * factor * gain_ref[...].astype(jnp.float32)).astype(jnp.bfloat16)
+
+    slot_row = slot_ref[...]
+    index_col = lax.broadcasted_iota(jnp.int32, (tokens, 1), 0).astype(jnp.float32)
+    slot_col = jnp.zeros((tokens, 1), jnp.float32)
+    start_col = jnp.zeros((tokens, 1), jnp.float32)
+    adapter_col = jnp.zeros((tokens, 1), jnp.int32) + adapter_ref[0]
+    for r in range(1, 4):
+        start = jnp.sum(jnp.where(slot_row < r, 1.0, 0.0), axis=1, keepdims=True)
+        reached = index_col >= start
+        slot_col = jnp.where(reached, float(r), slot_col)
+        start_col = jnp.where(reached, start, start_col)
+        adapter_col = jnp.where(reached, adapter_ref[r], adapter_col)
+    position = index_col - start_col + float(PROMPT_LENGTH)
+    lane = lax.broadcasted_iota(jnp.int32, (1, HEAD_WIDTH), 1)
+    pair = lax.rem(lane, HEAD_WIDTH // 2).astype(jnp.float32)
+    frequency = jnp.exp(pair * (-math.log(THETA) / (HEAD_WIDTH // 2)))
+    angle = position * frequency
+    cos_s[...] = jnp.cos(angle)
+    sin_s[...] = jnp.where(lane < HEAD_WIDTH // 2, -jnp.sin(angle), jnp.sin(angle))
+
+    def rotate(v):
+        return v * cos_s[...] + pltpu.roll(v, HEAD_WIDTH // 2, 1) * sin_s[...]
+
+    for g in groups:
+        ring1[g].pass_on()
+
+    weights[0].wait()
+    kv = jnp.dot(normed[...], wkv[...], preferred_element_type=jnp.float32)
+    for h in range(2):
+        k_s[h] = rotate(kv[:, h * 128:(h + 1) * 128]).astype(jnp.bfloat16)
+        v_s[h] = kv[:, 256 + h * 128:256 + (h + 1) * 128].astype(jnp.bfloat16)
+
+    for g in groups:
+        ring1[g].finish()
+        ring2[g].begin()
+        ring3[g][0].begin()
+
+    owner = lax.broadcasted_iota(jnp.int32, (tokens, aqd.shape[1]), 1) // ADAPTER_RANK
+    mine = owner == adapter_col
+    weights[1].wait()
+    inner = jnp.dot(normed[...], aqd[...], preferred_element_type=jnp.float32)
+    inner_s[...] = jnp.where(mine, inner, 0.0).astype(jnp.bfloat16)
+    weights[2].wait()
+    weights[3].wait()
+
+    def queries(lo, hi):
+        @pl.loop(lo, hi)
+        def _(n):
+            cols = pl.ds(pl.multiple_of(n * 256, 256), 256)
+            qv = jnp.dot(normed[...], wq[:, cols], preferred_element_type=jnp.float32)
+            qv = qv + jnp.dot(inner_s[...], aqu[:, cols], preferred_element_type=jnp.float32)
+            for h in range(2):
+                q_s[n * 2 + h] = rotate(qv[:, h * 128:(h + 1) * 128]).astype(jnp.bfloat16)
+
+    queries(0, 3)
+    for g in groups:
+        ring2[g].pass_on()
+        ring3[g][3].begin()
+        ring3[g][1].begin()
+    queries(3, 6)
+    for g in groups:
+        ring3[g][0].pass_on()
+        ring2[g].finish()
+        ring3[g][2].begin()
+        share_mine(g, 0).start()
+    for o, before in ((3, 0), (1, 3), (2, 1)):
+        for g in groups:
+            ring3[g][o].pass_on()
+            ring3[g][before].finish()
+            for third in range(3):
+                share_mine(g, 1 + before * 3 + third).start()
+    for g in groups:
+        ring3[g][2].finish()
+        for third in range(3):
+            share_mine(g, 1 + 2 * 3 + third).start()
+    for g in groups:
+        for i in range(13):
+            theirs(g, i).wait_recv()
+
+    @pl.loop(0, 4)
+    def _(r):
+        base = prompt_ref[r] * PPP
+        for j in range(PPP):
+            page = table_ref[base + j]
+            d = page // 4
+            px, py, pz, pc = d // 32, lax.rem(d // 8, 4), lax.rem(d // 2, 4), lax.rem(d, 2)
+            t = lax.rem(page, 4) * 4
+            for col in range(4):
+                kv_s[col, r, pl.ds(j * 16, 16), :] = cache[px, py, pz, pc, t + col]
+
+    scale = HEAD_WIDTH ** (-0.5)
+    group = QUERY_HEADS // KEY_VALUE_HEADS
+    nt = (((1,), (1,)), ((), ()))
+
+    @pl.loop(0, KEY_VALUE_HEADS)
+    def _(h):
+        for b in range(2):
+            rows = slice(b * half_rows, (b + 1) * half_rows)
+            keys = (b + 1) * half_rows
+            q = q_s[pl.ds(h * group, group), rows, :].reshape(group * half_rows, HEAD_WIDTH)
+            slot = slot_col[rows]
+            ki = lax.broadcasted_iota(jnp.int32, (half_rows, keys), 1).astype(jnp.float32)
+            ok = jnp.logical_and(ki <= index_col[rows], ki >= start_col[rows])
+            local = lax.dot_general(q, k_s[h, 0:keys], nt, preferred_element_type=jnp.float32)
+            local = local.reshape(group, half_rows, keys) * scale
+            local = jnp.where(ok[None], local, VERY_NEGATIVE)
+            picked = None
+            for r in range(b, b + 3):
+                s = lax.dot_general(q, kv_s[h, r], nt, preferred_element_type=jnp.float32)
+                s = s.reshape(group, half_rows, PROMPT_LENGTH)
+                picked = s if picked is None else jnp.where((slot == float(r))[None], s, picked)
+            picked = picked * scale
+            top = jnp.maximum(jnp.max(picked, axis=-1, keepdims=True), jnp.max(local, axis=-1, keepdims=True))
+            wp = jnp.exp(picked - top)
+            wl = jnp.exp(local - top)
+            total = jnp.sum(wp, axis=-1, keepdims=True) + jnp.sum(wl, axis=-1, keepdims=True)
+            wp = wp.astype(jnp.bfloat16).reshape(group * half_rows, PROMPT_LENGTH)
+            wl = wl.astype(jnp.bfloat16).reshape(group * half_rows, keys)
+            summed = None
+            for r in range(b, b + 3):
+                o = jnp.dot(wp, kv_s[KEY_VALUE_HEADS + h, r], preferred_element_type=jnp.float32)
+                o = o.reshape(group, half_rows, HEAD_WIDTH)
+                summed = o if summed is None else jnp.where((slot == float(r))[None], o, summed)
+            o = jnp.dot(wl, v_s[h, 0:keys], preferred_element_type=jnp.float32)
+            summed = (summed + o.reshape(group, half_rows, HEAD_WIDTH)) / total
+            for i in range(group):
+                col = pl.multiple_of((h * group + i) * HEAD_WIDTH, HEAD_WIDTH)
+                att[rows, pl.ds(col, HEAD_WIDTH)] = summed[i].astype(jnp.bfloat16)
+
+    for cp in weights[4:]:
+        cp.wait()
+    inner = jnp.dot(att[...], aod[...], preferred_element_type=jnp.float32)
+    inner_s[...] = jnp.where(mine, inner, 0.0).astype(jnp.bfloat16)
+
+    @pl.loop(0, width // 512)
+    def _(n):
+        cols = pl.ds(pl.multiple_of(n * 512, 512), 512)
+        mix = jnp.dot(att[...], wo[:, cols], preferred_element_type=jnp.float32)
+        mix = mix + jnp.dot(inner_s[...], aou[:, cols], preferred_element_type=jnp.float32)
+        hid_ref[:, cols] = (tokens_ref[:, cols].astype(jnp.float32) + mix).astype(jnp.bfloat16)
+
+    for g in groups:
+        ring1[g].drain()
+        ring2[g].drain()
+        for o in range(4):
+            ring3[g][o].drain()
+        for i in range(13):
+            share_mine(g, i).wait_send()
+
+
+def front(slots, prompts, adapters, table, tokens, shard, gain, wq, wkv, wo, aqd, aqu, aod, aou):
+    rows, width = tokens.shape
+    bf, f32 = jnp.bfloat16, jnp.float32
+    dma = pltpu.SemaphoreType.DMA
+    vmem = pl.BlockSpec(memory_space=pltpu.VMEM)
+    smem = pl.BlockSpec(memory_space=pltpu.SMEM)
+    hbm = pl.BlockSpec(memory_space=pl.ANY)
+    ordered = (wq, wkv, aqd, aqu, wo, aod, aou)
+    return pl.pallas_call(
+        front_kernel,
+        out_shape=jax.ShapeDtypeStruct((rows, width), bf),
+        in_specs=[vmem, smem, smem, smem, vmem, hbm, vmem] + [hbm] * 7,
+        out_specs=vmem,
+        scratch_shapes=[pltpu.VMEM((4, 4, 4, 2, 16, 16, 128), bf)]
+        + [pltpu.VMEM(w.shape, bf) for w in ordered]
+        + [
+            pltpu.VMEM((rows, width), bf),
+            pltpu.VMEM((rows, aqd.shape[1]), bf),
+            pltpu.VMEM((rows, HEAD_WIDTH), f32),
+            pltpu.VMEM((rows, HEAD_WIDTH), f32),
+            pltpu.VMEM((QUERY_HEADS, rows, HEAD_WIDTH), bf),
+            pltpu.VMEM((KEY_VALUE_HEADS, rows, HEAD_WIDTH), bf),
+            pltpu.VMEM((KEY_VALUE_HEADS, rows, HEAD_WIDTH), bf),
+            pltpu.VMEM((2 * KEY_VALUE_HEADS, 4, PROMPT_LENGTH, HEAD_WIDTH), bf),
+            pltpu.VMEM((rows, width), bf),
+            dma((7,)), dma((16,)), dma((3, 6, 4)), dma((3, 6, 4)), dma((3, 13)), dma((3, 13)),
+        ],
+        compiler_params=pltpu.CompilerParams(
+            collective_id=2, has_side_effects=True, vmem_limit_bytes=60 * 1024 * 1024),
+        name="front",
+    )(slots, prompts, adapters, table, tokens, shard, gain.reshape(1, width), *ordered)
 
 
 def moe_kernel(
@@ -408,64 +628,10 @@
     expert_gate_up,
     expert_down,
 ):
-    new_token_count = tokens.shape[0]
-    request_row = token_request_slot[0]
-    request_slot_count = request_prompt.shape[0]
-    token_adapter, prompt_tok, token_positions = request_info(
-        request_row, request_prompt, request_adapter
-    )
-    query_rows, key_matrix, value_matrix = apply_projection(
-        tokens,
-        token_adapter,
-        token_positions,
-        attention_norm_gain,
-        query_matrix,
-        key_value_weight,
-        adapter_query_down,
-        adapter_query_up,
-    )
-    query_group_width = QUERY_HEADS // KEY_VALUE_HEADS
-    grouped_queries = query_rows.reshape(
-        new_token_count, KEY_VALUE_HEADS, query_group_width, HEAD_WIDTH
-    )
-    token_index = jnp.arange(new_token_count, dtype=jnp.int32)
-    local_ok = (request_row[:, None] == request_row[None, :]) & (
-        token_index[None, :] <= token_index[:, None]
-    )
-    initial = (
-        jnp.full((new_token_count, KEY_VALUE_HEADS, query_group_width), VERY_NEGATIVE, jnp.float32),
-        jnp.zeros((new_token_count, KEY_VALUE_HEADS, query_group_width), jnp.float32),
-        jnp.zeros((new_token_count, KEY_VALUE_HEADS, query_group_width, HEAD_WIDTH), jnp.float32),
-    )
-    running_progress = block_attention(initial, grouped_queries, key_matrix, value_matrix, local_ok)
-    requested_pages = jnp.take(prompt_page_table.reshape(-1, PPP), request_prompt, axis=0).reshape(
-        -1
-    )
-    complete_cache = lax.all_gather(shared_prompt_cache, ("req", "exp"), axis=0, tiled=True)
-    page_token_rows = jnp.take(complete_cache, requested_pages, axis=0).reshape(
-        request_slot_count * PROMPT_LENGTH, 2 * KEY_VALUE_HEADS, HEAD_WIDTH
-    )
-    owner_slot = jnp.arange(request_slot_count * PROMPT_LENGTH, dtype=jnp.int32) // PROMPT_LENGTH
-    prompt_valid_mask = request_row[:, None] == owner_slot[None, :]
-    running_progress = block_attention(
-        running_progress,
-        grouped_queries,
-        page_token_rows[:, :KEY_VALUE_HEADS],
-        page_token_rows[:, KEY_VALUE_HEADS:],
-        prompt_valid_mask,
-    )
-    running_max, totals, accum = running_progress
-    attention_output = (
-        (accum / totals[..., None])
-        .reshape(new_token_count, QUERY_HEADS * HEAD_WIDTH)
-        .astype(jnp.bfloat16)
-    )
-    hidden_state = finalize(
-        attention_output,
-        tokens,
-        token_adapter,
-        attention_output_weight,
-        adapter_output_down,
+    hidden_state = front(
+        token_request_slot, request_prompt, request_adapter, prompt_page_table, tokens,
+        shared_prompt_cache, attention_norm_gain, query_matrix, key_value_weight,
+        attention_output_weight, adapter_query_down, adapter_query_up, adapter_output_down,
         adapter_output_up,
     )
     return moe(hidden_state, expert_norm_gain, routes, router, expert_gate_up, expert_down)

time: 217 us -> 155 us (0.71)
  Pallas kernels: 94.6 us -> 149 us
  waiting for transfers between devices: 42.6 us -> 0 us
  matrix products: 29.2 us -> 0 us
  local copies, waits for them, and re-layouts: 22.1 us -> 5.91 us
  other arithmetic: 13.9 us -> 0 us
  between operations: 13.7 us -> 0.02 us
    pallas_call x0 -> x1, Pallas kernels: none -> 53.5 us  [front(): pl.pallas_call(front_kernel, out_shape=jax.ShapeDtypeStruct((rows, width)...]
    all_gather x1 -> x0, waiting for transfers between devices: 41.9 us -> none  [on_device(): lax.all_gather(shared_prompt_cache, ('req', 'exp'), axis=0, tiled=True)]
    dot_general x9 -> x0, matrix products: 29.2 us -> none  [the longest x2 8.01 us: adapter_update(): return jnp.dot(inner, up_proj, preferred_element_type=jnp.float32)]
    gather x3 -> x0, local copies, waits for them, and re-layouts: 7.66 us -> none  [the longest x2 7.1 us: on_device(): jnp.take(complete_cache, requested_pages, axis=0)]
    reduce_sum x4 -> x0, other arithmetic: 5.36 us -> none  [the longest x2 3.21 us: block_attention(): totals = totals * factor + jnp.sum(weights, axis=-1)]
    another operation x3 -> x0, other arithmetic: 2.97 us -> none
    select_n x6 -> x0, other arithmetic: 2.78 us -> none  [the longest x2 2.04 us: on_device(): jnp.take(complete_cache, requested_pages, axis=0)]
  transfers between devices with their start and end apart: 1 -> 0, of which waited for: 1 -> 0; matrix products, arithmetic and copies ran while one was open for 16% -> 0% of each run, Pallas kernels for 0% -> 0%
where the time goes in v2:
time: 155 us
  Pallas kernels  149 us (96%)
  local copies, waits for them, and re-layouts  5.91 us (4%)
    pallas_call x1, Pallas kernels, moe(): pl.pallas_call(moe_kernel, out_shape=jax.ShapeDtypeStruct((tokens, width)...  95.4 us
    pallas_call x1, Pallas kernels, front(): pl.pallas_call(front_kernel, out_shape=jax.ShapeDtypeStruct((rows, width)...  53.5 us

profile of v2, /device:TPU:1, one launch (start us, length us, event | category | flops | bytes accessed | tf_op | source)
XLA Modules:
  0.0 154.8 jit_solution(12604879922815043799)
XLA Ops:
  0.0 1.3 reshape.12.gain_ref
  1.3 1.3 reshape.13.gain_ref
  2.6 1.3 concatenate.3.routes_ref
  3.9 53.5 %front.1.hid_ref = bf16[256,1536]{1,0:T(8,128)(2,1)} custom-call(s32[1,256]{1,0:T(1,128)} %slot_ref.1, s32[4]{0:T(128)} %prompt_ref.1, s32[4]{0:T(128)} %adapter_ref.1, s32[512]{0:T(512)} %table_ref.1, bf16[256,1536]{1,0:T(8,128)(2,1)} %tokens_ref.1, bf16[4,16,512]{2,1,0:T(8,128)(2,1)} %cache_ref.1, bf16[1,1536]{1,0:T(2,128)(2,1)} %reshape.12.gain_ref, ...), custom_call_target="tpu_custom_call" | custom-call | tf_op jit(solution)/shard_map/front/pallas_call | solution.py:333
  57.3 95.4 %moe.1 = bf16[256,1536]{1,0:T(8,128)(2,1)} custom-call(bf16[256,1536]{1,0:T(8,128)(2,1)} %front.1.hid_ref, bf16[1,1536]{1,0:T(2,128)(2,1)} %reshape.13.gain_ref, s32[8,256]{1,0:T(8,128)} %concatenate.3.routes_ref, bf16[32,1536]{1,0:T(8,128)(2,1)} %bitcast.6, bf16[1536,1536]{1,0:T(8,128)(2,1)} %bitcast.4, bf16[768,1536]{1,0:T(8,128)(2,1)} %bitcast.5), custom_call_target="tpu_custom_call" | custom-call | tf_op jit(solution)/shard_map/moe/pallas_call | solution.py:580
  152.8 2.1 %copy.21 = bf16[256,1536]{1,0:T(8,128)(2,1)} copy(bf16[256,1536]{1,0:T(8,128)(2,1)} %moe.1) | data formatting | bytes 1572864

commit v3 on v2

v3 whole, which is shorter than its diff:
```python
import math

import jax
import jax.numpy as jnp
from jax import lax
from jax.experimental import pallas as pl
from jax.experimental.pallas import tpu as pltpu
from jax.sharding import PartitionSpec as P

MESH = pl.DeviceIdType.MESH
CAP = 48
FFE = 768

QUERY_HEADS = 12
KEY_VALUE_HEADS = 2
HEAD_WIDTH = 128
TOPK = 4
ADAPTER_RANK = 16
PPP = 16
PROMPT_LENGTH = 256


EPSILON = 1e-06
THETA = 1000000.0
VERY_NEGATIVE = -1e30


TILE_GROUPS = ((0, 6), (6, 5), (11, 5))
AXIS_ORDERS = ((0, 1, 2), (1, 2, 0), (2, 0, 1))


def layer_kernel(
    slot_ref, prompt_ref, adapter_ref, table_ref, tokens_ref, cache_ref, gain_ref,
    routes_ref, expert_gain_ref, router_ref,
    wq_any, wkv_any, aqd_any, aqu_any, wo_any, aod_any, aou_any, wgu_any, wdn_any,
    out_ref,
    cache, wq, wkv, aqd, aqu, wo, aod, aou, wgu_ref, wdn_ref,
    normed, inner_s, cos_s, sin_s, q_s, k_s, v_s, kv_s, att,
    xbuf, rbuf, rank_s, gate_s, ct_s, arrived, units, returned, psend, precv, acc,
    w_sem, c_sem, ag_s, ag_r, co_s, co_r,
    sa_x, ra_x, sa_r, ra_r, sb_p, rb_p, sb_r, rb_r, sp_s, sp_r,
):
    pack, result = wo, wq
    x = lax.axis_index("req")
    e_me = lax.axis_index("exp")
    y = e_me // 8
    z = lax.rem(e_me // 2, 4)
    c = lax.rem(e_me, 2)
    here = (x, y, z)

    def device(axis, offset):
        p = list(here)
        p[axis] = lax.rem(p[axis] + offset, 4)
        return (p[0], (p[1] * 4 + p[2]) * 2 + c)

    partner = (x, (y * 4 + z) * 2 + 1 - c)

    barrier = pltpu.get_barrier_semaphore()
    for off in (1, 2, 3):
        pl.semaphore_signal(barrier, 1, device_id=device(0, off), device_id_type=MESH)
    for dy in range(4):
        for dc in range(2):
            if dy or dc:
                dev = (x, (lax.rem(y + dy, 4) * 4 + z) * 2 + lax.rem(c + dc, 2))
                pl.semaphore_signal(barrier, 1, device_id=dev, device_id_type=MESH)
    for dz in range(1, 4):
        for dc in range(2):
            dev = (x, (y * 4 + lax.rem(z + dz, 4)) * 2 + lax.rem(c + dc, 2))
            pl.semaphore_signal(barrier, 1, device_id=dev, device_id_type=MESH)

    first_pos = y * (1 - c) + z * c
    first_base = z * 2 * (1 - c) + y * 8 * c + c
    first_step = 8 - 6 * c
    second_pos = z * (1 - c) + y * c
    second_base = y * 8 * (1 - c) + z * 2 * c
    second_step = 2 + 6 * c

    def first_dev(offset):
        return (x, first_base + lax.rem(first_pos + offset, 4) * first_step)

    def second_exp(offset, dc):
        return second_base + lax.rem(second_pos + offset, 4) * second_step + lax.rem(c + dc, 2)

    def relay_dev(j, dc):
        rc = lax.rem(c + dc, 2)
        pos = z * (1 - rc) + y * rc
        base = y * 8 * (1 - rc) + z * 2 * rc
        return (x, base + lax.rem(pos - j + 4, 4) * (2 + 6 * rc) + rc)

    def remote(src, dst, ssem, rsem, dev):
        return pltpu.make_async_remote_copy(
            src_ref=src, dst_ref=dst, send_sem=ssem, recv_sem=rsem,
            device_id=dev, device_id_type=MESH)

    own = []
    for p in range(4):
        for col in range(4):
            cp = pltpu.make_async_copy(
                cache_ref.at[p, :, pl.ds(col * 128, 128)],
                cache.at[x, y, z, c, p * 4 + col], c_sem.at[p * 4 + col])
            cp.start()
            own.append(cp)
    weights = []
    for i, (src, dst) in enumerate((
            (wkv_any, wkv), (aqd_any, aqd), (aqu_any, aqu), (wq_any, wq),
            (aod_any, aod), (wo_any, wo), (aou_any, aou), (wgu_any, wgu_ref), (wdn_any, wdn_ref))):
        cp = pltpu.make_async_copy(src, dst, w_sem.at[i])
        cp.start()
        weights.append(cp)

    def block(where, first, count):
        return cache.at[where[0], where[1], where[2], c, pl.ds(first, count)]

    def step(g, phase, kind, axis, where):
        lo, n = TILE_GROUPS[g]
        if kind == 2:
            n = n // 2
        elif kind == 3:
            lo, n = lo + n // 2, n - n // 2
        view = block(where, lo, n)
        return pltpu.make_async_remote_copy(
            src_ref=view, dst_ref=view, send_sem=ag_s.at[g, phase, kind], recv_sem=ag_r.at[g, phase, kind],
            device_id=device(axis, {0: 1, 2: 1, 4: 2}.get(kind, 3)), device_id_type=MESH)

    every = slice(None)

    def place(g, second, third):
        order = AXIS_ORDERS[g]
        w = [every, every, every]
        for axis, off in ((order[1], second), (order[2], third)):
            if off is not None:
                w[axis] = lax.rem(here[axis] + off, 4)
        return w

    class Ring:
        def __init__(self, g, phase, axis, where_of):
            self.g, self.phase, self.axis, self.where_of = g, phase, axis, where_of

        def cp(self, kind, off):
            return step(self.g, self.phase, kind, self.axis, self.where_of(off))

        def begin(self):
            self.cp(0, 0).start()
            self.cp(1, 0).start()

        def pass_on(self):
            self.cp(0, 3).wait_recv()
            self.cp(2, 3).start()
            self.cp(1, 1).wait_recv()
            self.cp(3, 1).start()

        def finish(self):
            self.cp(2, 2).wait_recv()
            self.cp(3, 2).wait_recv()

        def drain(self):
            self.cp(0, 0).wait_send()
            self.cp(1, 0).wait_send()
            self.cp(2, 3).wait_send()
            self.cp(3, 1).wait_send()

    class Short(Ring):
        def begin(self):
            for kind in (0, 1, 4):
                self.cp(kind, 0).start()

        def near(self):
            self.cp(0, 3).wait_recv()
            self.cp(1, 1).wait_recv()

        def finish(self):
            self.cp(4, 2).wait_recv()

        def drain(self):
            for kind in (0, 1, 4):
                self.cp(kind, 0).wait_send()

    def first_where(g):
        def f(off):
            order = AXIS_ORDERS[g]
            w = [here[0], here[1], here[2]]
            w[order[0]] = lax.rem(here[order[0]] + off, 4)
            return w
        return f

    groups = range(3)
    ring1 = [Short(g, 0, AXIS_ORDERS[g][0], first_where(g)) for g in groups]
    ring2 = [Short(g, 1, AXIS_ORDERS[g][1], lambda off, g=g: place(g, off, 0)) for g in groups]
    ring3 = [[Ring(g, 2 + o, AXIS_ORDERS[g][2], lambda off, g=g, o=o: place(g, o, off)) for o in range(4)]
             for g in groups]

    def share(g, i, second, third):
        lo, n = TILE_GROUPS[g]
        view = block(place(g, second, third), lo, n)
        return pltpu.make_async_remote_copy(
            src_ref=view, dst_ref=view, send_sem=co_s.at[g, i], recv_sem=co_r.at[g, i],
            device_id=partner, device_id_type=MESH)

    def share_mine(g, i):
        if i == 0:
            return share(g, 0, None, 0)
        return share(g, i, (i - 1) // 3, 1 + (i - 1) % 3)

    def theirs(g, i):
        lo, n = TILE_GROUPS[g]
        second, third = (None, 0) if i == 0 else ((i - 1) // 3, 1 + (i - 1) % 3)
        w = place(g, second, third)
        view = cache.at[w[0], w[1], w[2], 1 - c, pl.ds(lo, n)]
        return pltpu.make_async_remote_copy(
            src_ref=view, dst_ref=view, send_sem=co_s.at[g, i], recv_sem=co_r.at[g, i],
            device_id=partner, device_id_type=MESH)

    tokens = tokens_ref.shape[0]
    width = tokens_ref.shape[1]
    half_rows = tokens // 2

    tv = tokens_ref[...].astype(jnp.float32)
    factor = lax.rsqrt(jnp.mean(tv * tv, axis=-1, keepdims=True) + EPSILON)
    gain = gain_ref[...].astype(jnp.float32).reshape(1, width)
    normed[...] = (tv * factor * gain).astype(jnp.bfloat16)

    for cp in own:
        cp.wait()
    pl.semaphore_wait(barrier, 16)
    for g in groups:
        ring1[g].begin()

    slot_row = slot_ref[...]
    index_col = lax.broadcasted_iota(jnp.int32, (tokens, 1), 0).astype(jnp.float32)
    slot_col = jnp.zeros((tokens, 1), jnp.float32)
    start_col = jnp.zeros((tokens, 1), jnp.float32)
    adapter_col = jnp.zeros((tokens, 1), jnp.int32) + adapter_ref[0]
    for r in range(1, 4):
        start = jnp.sum(jnp.where(slot_row < r, 1.0, 0.0), axis=1, keepdims=True)
        reached = index_col >= start
        slot_col = jnp.where(reached, float(r), slot_col)
        start_col = jnp.where(reached, start, start_col)
        adapter_col = jnp.where(reached, adapter_ref[r], adapter_col)
    position = index_col - start_col + float(PROMPT_LENGTH)
    lane = lax.broadcasted_iota(jnp.int32, (1, HEAD_WIDTH), 1)
    pair = lax.rem(lane, HEAD_WIDTH // 2).astype(jnp.float32)
    frequency = jnp.exp(pair * (-math.log(THETA) / (HEAD_WIDTH // 2)))
    angle = position * frequency
    cos_s[...] = jnp.cos(angle)
    sin_s[...] = jnp.where(lane < HEAD_WIDTH // 2, -jnp.sin(angle), jnp.sin(angle))

    def rotate(v):
        return v * cos_s[...] + pltpu.roll(v, HEAD_WIDTH // 2, 1) * sin_s[...]

    for g in groups:
        ring1[g].near()
        ring1[g].finish()
        ring2[g].begin()
    for g in groups:
        ring3[g][0].begin()

    weights[0].wait()
    kv = jnp.dot(normed[...], wkv[...], preferred_element_type=jnp.float32)
    for h in range(2):
        k_s[h] = rotate(kv[:, h * 128:(h + 1) * 128]).astype(jnp.bfloat16)
        v_s[h] = kv[:, 256 + h * 128:256 + (h + 1) * 128].astype(jnp.bfloat16)

    for g in groups:
        ring2[g].near()
        ring3[g][3].begin()
        ring3[g][1].begin()
    for g in groups:
        ring2[g].finish()
        ring3[g][2].begin()
        share_mine(g, 0).start()

    owner = lax.broadcasted_iota(jnp.int32, (tokens, aqd.shape[1]), 1) // ADAPTER_RANK
    mine = owner == adapter_col
    weights[1].wait()
    inner = jnp.dot(normed[...], aqd[...], preferred_element_type=jnp.float32)
    inner_s[...] = jnp.where(mine, inner, 0.0).astype(jnp.bfloat16)
    weights[2].wait()
    weights[3].wait()

    def queries(lo, hi):
        @pl.loop(lo, hi)
        def _(n):
            cols = pl.ds(pl.multiple_of(n * 256, 256), 256)
            qv = jnp.dot(normed[...], wq[:, cols], preferred_element_type=jnp.float32)
            qv = qv + jnp.dot(inner_s[...], aqu[:, cols], preferred_element_type=jnp.float32)
            for h in range(2):
                q_s[n * 2 + h] = rotate(qv[:, h * 128:(h + 1) * 128]).astype(jnp.bfloat16)

    queries(0, 3)
    for g in groups:
        ring3[g][0].pass_on()
        for third in (0, 2):
            share_mine(g, 1 + third).start()
    queries(3, 6)

    row_i = lax.broadcasted_iota(jnp.int32, (tokens, tokens), 0)
    col_i = lax.broadcasted_iota(jnp.int32, (tokens, tokens), 1)
    eye = jnp.where(row_i == col_i, 1.0, 0.0).astype(jnp.bfloat16)
    rbuf[0] = jnp.full(rbuf.shape[1:], -1.0, jnp.float32)
    rbuf[0, 0:TOPK, :] = lax.dot_general(
        routes_ref[...].astype(jnp.float32).astype(jnp.bfloat16), eye, (((0,), (0,)), ((), ())),
        preferred_element_type=jnp.float32)

    for o, before in ((3, 0), (1, 3), (2, 1)):
        for g in groups:
            ring3[g][o].pass_on()
            for third in (0, 2):
                share_mine(g, 1 + o * 3 + third).start()
            ring3[g][before].finish()
            share_mine(g, 1 + before * 3 + 1).start()
    r_copies = []
    for i, off in ((1, 1), (2, 3), (3, 2)):
        cp = remote(rbuf.at[0], rbuf.at[i], sa_r.at[i], ra_r.at[i], first_dev(off))
        cp.start()
        r_copies.append(cp)
    for g in groups:
        ring3[g][2].finish()
        share_mine(g, 1 + 2 * 3 + 1).start()
    for g in groups:
        for i in range(13):
            theirs(g, i).wait_recv()

    @pl.loop(0, 4)
    def _(r):
        base = prompt_ref[r] * PPP
        for j in range(PPP):
            page = table_ref[base + j]
            d = page // 4
            px, py, pz, pc = d // 32, lax.rem(d // 8, 4), lax.rem(d // 2, 4), lax.rem(d, 2)
            t = lax.rem(page, 4) * 4
            for col in range(4):
                kv_s[col, r, pl.ds(j * 16, 16), :] = cache[px, py, pz, pc, t + col]

    scale = HEAD_WIDTH ** (-0.5)
    group = QUERY_HEADS // KEY_VALUE_HEADS
    nt = (((1,), (1,)), ((), ()))

    before_m = jnp.where(row_i < col_i, 1.0, 0.0).astype(jnp.bfloat16)
    half = half_rows
    offsets = (0, 1, 3, 2)

    def x_copy(i, h):
        rows = pl.ds(h * half, half)
        return remote(xbuf.at[0, rows], xbuf.at[i, rows], sa_x.at[i, h], ra_x.at[i, h],
                      first_dev(offsets[i]))

    def attend(b):
        @pl.loop(0, KEY_VALUE_HEADS)
        def _(h):
            rows = slice(b * half_rows, (b + 1) * half_rows)
            keys = (b + 1) * half_rows
            q = q_s[pl.ds(h * group, group), rows, :].reshape(group * half_rows, HEAD_WIDTH)
            slot = slot_col[rows]
            ki = lax.broadcasted_iota(jnp.int32, (half_rows, keys), 1).astype(jnp.float32)
            ok = jnp.logical_and(ki <= index_col[rows], ki >= start_col[rows])
            local = lax.dot_general(q, k_s[h, 0:keys], nt, preferred_element_type=jnp.float32)
            local = local.reshape(group, half_rows, keys) * scale
            local = jnp.where(ok[None], local, VERY_NEGATIVE)
            picked = None
            for r in range(b, b + 3):
                s = lax.dot_general(q, kv_s[h, r], nt, preferred_element_type=jnp.float32)
                s = s.reshape(group, half_rows, PROMPT_LENGTH)
                picked = s if picked is None else jnp.where((slot == float(r))[None], s, picked)
            picked = picked * scale
            top = jnp.maximum(jnp.max(picked, axis=-1, keepdims=True), jnp.max(local, axis=-1, keepdims=True))
            wp = jnp.exp(picked - top)
            wl = jnp.exp(local - top)
            total = jnp.sum(wp, axis=-1, keepdims=True) + jnp.sum(wl, axis=-1, keepdims=True)
            wp = wp.astype(jnp.bfloat16).reshape(group * half_rows, PROMPT_LENGTH)
            wl = wl.astype(jnp.bfloat16).reshape(group * half_rows, keys)
            summed = None
            for r in range(b, b + 3):
                o = jnp.dot(wp, kv_s[KEY_VALUE_HEADS + h, r], preferred_element_type=jnp.float32)
                o = o.reshape(group, half_rows, HEAD_WIDTH)
                summed = o if summed is None else jnp.where((slot == float(r))[None], o, summed)
            o = jnp.dot(wl, v_s[h, 0:keys], preferred_element_type=jnp.float32)
            summed = (summed + o.reshape(group, half_rows, HEAD_WIDTH)) / total
            for i in range(group):
                col = pl.multiple_of((h * group + i) * HEAD_WIDTH, HEAD_WIDTH)
                att[rows, pl.ds(col, HEAD_WIDTH)] = summed[i].astype(jnp.bfloat16)

    def project(b):
        rows = slice(b * half_rows, (b + 1) * half_rows)
        inner = jnp.dot(att[rows], aod[...], preferred_element_type=jnp.float32)
        inner_s[rows] = jnp.where(mine[rows], inner, 0.0).astype(jnp.bfloat16)

        @pl.loop(0, width // 512)
        def _(n):
            cols = pl.ds(pl.multiple_of(n * 512, 512), 512)
            mix = jnp.dot(att[rows], wo[:, cols], preferred_element_type=jnp.float32)
            mix = mix + jnp.dot(inner_s[rows], aou[:, cols], preferred_element_type=jnp.float32)
            hid = (tokens_ref[rows, cols].astype(jnp.float32) + mix).astype(jnp.bfloat16)
            acc[rows, cols] = hid.astype(jnp.float32)

        hv = acc[rows]
        factor = lax.rsqrt(jnp.mean(hv * hv, axis=-1, keepdims=True) + EPSILON)
        xbuf[0, rows] = (hv * factor * expert_gain).astype(jnp.bfloat16)

    expert_gain = expert_gain_ref[...].astype(jnp.float32).reshape(1, width)
    attend(0)
    for cp in weights[4:7]:
        cp.wait()
    for b in range(2):
        if b:
            attend(b)
        project(b)
        x_copy(1, b).start()
        x_copy(2, b).start()

    experts = router_ref.shape[0]

    def make_tables(i):
        r = rbuf[i]
        ei = lax.broadcasted_iota(jnp.int32, (experts, tokens), 0).astype(jnp.float32)
        hit = ei == r[0:1, :]
        for k in range(1, TOPK):
            hit = jnp.logical_or(hit, ei == r[k:k + 1, :])
        hit_f = jnp.where(hit, 1.0, 0.0)
        rank = jnp.dot(hit_f.astype(jnp.bfloat16), before_m, preferred_element_type=jnp.float32)
        rank_s[i] = jnp.where(hit, rank, -1.0)
        logits = lax.dot_general(router_ref[...], xbuf[i], (((1,), (1,)), ((), ())),
                                 preferred_element_type=jnp.float32)
        sig = jnp.where(hit, jax.nn.sigmoid(logits), 0.0)
        gate_s[i] = sig / jnp.sum(sig, axis=0, keepdims=True)

    slot_i = lax.broadcasted_iota(jnp.int32, (CAP, tokens), 0).astype(jnp.float32)
    tile = 512

    def dispatch(i):
        picks = []
        for j in range(4):
            for dc in range(2):
                e = second_exp(j, dc)
                rank_row = rank_s[i, pl.ds(e, 1), :]
                gate_row = gate_s[i, pl.ds(e, 1), :]
                eq = slot_i == rank_row
                picks.append(jnp.where(eq, 1.0, 0.0).astype(jnp.bfloat16))
                q = j * 2 + dc
                ct_s[i, q * CAP:(q + 1) * CAP, :] = jnp.where(eq, gate_row, 0.0).astype(jnp.bfloat16)
        pick = jnp.concatenate(picks, axis=0)

        @pl.loop(0, width // tile)
        def _(n):
            cols = pl.ds(pl.multiple_of(n * tile, tile), tile)
            rows = jnp.dot(pick, xbuf[i, :, cols], preferred_element_type=jnp.float32).astype(jnp.bfloat16)
            arrived[i, 0:CAP, cols] = rows[0:CAP]
            pack[i * 8 * CAP:(i + 1) * 8 * CAP, cols] = rows
        for q in range(1, 8):
            pack_copy(i, q).start()

    def pack_copy(i, q):
        j, dc = q // 2, q % 2
        return remote(pack.at[pl.ds((i * 8 + q) * CAP, CAP)], arrived.at[i, pl.ds(q * CAP, CAP)],
                      sb_p.at[i, q], rb_p.at[i, q], (x, second_exp(j, dc)))

    def result_copy(i, q):
        j, dc = q // 2, q % 2
        return remote(result.at[pl.ds((i * 8 + q) * CAP, CAP)], returned.at[i, pl.ds(q * CAP, CAP)],
                      sb_r.at[i, q], rb_r.at[i, q], relay_dev(j, dc))

    def expert(i):
        for q in range(1, 8):
            pack_copy(i, q).wait_recv()

        @pl.loop(0, FFE // 256)
        def _(n):
            up_cols = pl.ds(pl.multiple_of(FFE + n * 256, 256), 256)
            cols = pl.ds(pl.multiple_of(n * 256, 256), 256)
            a = arrived[i]
            g = jnp.dot(a, wgu_ref[:, cols], preferred_element_type=jnp.float32)
            u = jnp.dot(a, wgu_ref[:, up_cols], preferred_element_type=jnp.float32)
            units[:, cols] = (jnp.maximum(g, 0.0) * u).astype(jnp.bfloat16)

        @pl.loop(0, width // tile)
        def _(n):
            cols = pl.ds(pl.multiple_of(n * tile, tile), tile)
            rows = jnp.dot(units[...], wdn_ref[:, cols], preferred_element_type=jnp.float32).astype(jnp.bfloat16)
            returned[i, 0:CAP, cols] = rows[0:CAP]
            result[i * 8 * CAP:(i + 1) * 8 * CAP, cols] = rows
        for q in range(1, 8):
            result_copy(i, q).start()

    def partial_copy(i):
        return remote(psend.at[i - 1], precv.at[i - 1], sp_s.at[i - 1], sp_r.at[i - 1],
                      first_dev(4 - offsets[i]))

    def combine(i):
        for q in range(1, 8):
            result_copy(i, q).wait_recv()

        @pl.loop(0, width // tile)
        def _(n):
            cols = pl.ds(pl.multiple_of(n * tile, tile), tile)
            part = lax.dot_general(ct_s[i], returned[i, :, cols], (((0,), (0,)), ((), ())),
                                   preferred_element_type=jnp.float32)
            if i == 0:
                acc[:, cols] = acc[:, cols] + part
            else:
                psend[i - 1, :, cols] = part.astype(jnp.bfloat16)
        if i:
            partial_copy(i).start()

    def forward(i):
        h = 0 if i == 1 else 1
        rows = pl.ds(h * half, half)
        return remote(xbuf.at[i, rows], xbuf.at[3, rows], sa_x.at[3, h], ra_x.at[3, h],
                      first_dev(1 if i == 1 else 3))

    make_tables(0)
    dispatch(0)
    for cp in weights[7:]:
        cp.wait()
    x_copy(1, 0).wait_recv()
    forward(1).start()
    x_copy(2, 1).wait_recv()
    forward(2).start()
    for i in (1, 2, 3):
        r_copies[i - 1].wait_recv()
        if i == 3:
            forward(1).wait_recv()
            forward(2).wait_recv()
        else:
            x_copy(i, 1 if i == 1 else 0).wait_recv()
        make_tables(i)
        dispatch(i)
        expert(i - 1)
        if i >= 2:
            combine(i - 2)
    expert(3)
    combine(2)
    combine(3)
    for i in (1, 2, 3):
        partial_copy(i).wait_recv()
    out_ref[...] = (acc[...] + precv[0].astype(jnp.float32) + precv[1].astype(jnp.float32)
                    + precv[2].astype(jnp.float32)).astype(jnp.bfloat16)
    for cp in r_copies:
        cp.wait_send()
    for i in (1, 2):
        for h in range(2):
            x_copy(i, h).wait_send()
    forward(1).wait_send()
    forward(2).wait_send()
    for i in range(4):
        for q in range(1, 8):
            pack_copy(i, q).wait_send()
            result_copy(i, q).wait_send()
        if i:
            partial_copy(i).wait_send()
    for g in groups:
        ring1[g].drain()
        ring2[g].drain()
        for o in range(4):
            ring3[g][o].drain()
        for i in range(13):
            share_mine(g, i).wait_send()


def layer(slots, prompts, adapters, table, tokens, shard, gain, routes, expert_gain, router,
          wq, wkv, wo, aqd, aqu, aod, aou, wgu, wdn):
    rows, width = tokens.shape
    bf, f32 = jnp.bfloat16, jnp.float32
    dma = pltpu.SemaphoreType.DMA
    vmem = pl.BlockSpec(memory_space=pltpu.VMEM)
    smem = pl.BlockSpec(memory_space=pltpu.SMEM)
    hbm = pl.BlockSpec(memory_space=pl.ANY)
    experts = router.shape[1]
    ordered = (wq, wkv, aqd, aqu, wo, aod, aou, wgu.reshape(wgu.shape[-2:]), wdn.reshape(wdn.shape[-2:]))
    routed = 8 * CAP
    return pl.pallas_call(
        layer_kernel,
        out_shape=jax.ShapeDtypeStruct((rows, width), bf),
        in_specs=[vmem, smem, smem, smem, vmem, hbm, vmem, vmem, vmem, vmem] + [hbm] * 9,
        out_specs=vmem,
        scratch_shapes=[pltpu.VMEM((4, 4, 4, 2, 16, 16, 128), bf)]
        + [pltpu.VMEM(w.shape, bf) for w in ordered]
        + [
            pltpu.VMEM((rows, width), bf),
            pltpu.VMEM((rows, aqd.shape[1]), bf),
            pltpu.VMEM((rows, HEAD_WIDTH), f32),
            pltpu.VMEM((rows, HEAD_WIDTH), f32),
            pltpu.VMEM((QUERY_HEADS, rows, HEAD_WIDTH), bf),
            pltpu.VMEM((KEY_VALUE_HEADS, rows, HEAD_WIDTH), bf),
            pltpu.VMEM((KEY_VALUE_HEADS, rows, HEAD_WIDTH), bf),
            pltpu.VMEM((2 * KEY_VALUE_HEADS, 4, PROMPT_LENGTH, HEAD_WIDTH), bf),
            pltpu.VMEM((rows, width), bf),
            pltpu.VMEM((4, rows, width), bf),
            pltpu.VMEM((4, 8, rows), f32),
            pltpu.VMEM((4, experts, rows), f32),
            pltpu.VMEM((4, experts, rows), f32),
            pltpu.VMEM((4, routed, rows), bf),
            pltpu.VMEM((4, routed, width), bf),
            pltpu.VMEM((routed, FFE), bf),
            pltpu.VMEM((4, routed, width), bf),
            pltpu.VMEM((3, rows, width), bf),
            pltpu.VMEM((3, rows, width), bf),
            pltpu.VMEM((rows, width), f32),
            dma((9,)), dma((16,)), dma((3, 6, 5)), dma((3, 6, 5)), dma((3, 13)), dma((3, 13)),
            dma((4, 2)), dma((4, 2)), dma((4,)), dma((4,)),
            dma((4, 8)), dma((4, 8)), dma((4, 8)), dma((4, 8)),
            dma((3,)), dma((3,)),
        ],
        compiler_params=pltpu.CompilerParams(
            collective_id=1, has_side_effects=True, vmem_limit_bytes=63 * 1024 * 1024),
        name="layer",
    )(slots, prompts, adapters, table, tokens, shard, gain, routes, expert_gain, router.T, *ordered)


def on_device(
    tokens,
    token_request_slot,
    request_prompt,
    request_adapter,
    prompt_page_table,
    shared_prompt_cache,
    routes,
    attention_norm_gain,
    query_matrix,
    key_value_weight,
    attention_output_weight,
    adapter_query_down,
    adapter_query_up,
    adapter_output_down,
    adapter_output_up,
    expert_norm_gain,
    router,
    expert_gate_up,
    expert_down,
):
    return layer(
        token_request_slot, request_prompt, request_adapter, prompt_page_table, tokens,
        shared_prompt_cache, attention_norm_gain, routes, expert_norm_gain, router,
        query_matrix, key_value_weight, attention_output_weight, adapter_query_down,
        adapter_query_up, adapter_output_down, adapter_output_up, expert_gate_up, expert_down,
    )


def solution(mesh):
    return jax.shard_map(
        on_device,
        mesh=mesh,
        in_specs=(
            P(("req", "exp"), None),
            P(("req", "exp"), None),
            P(("req", "exp")),
            P(("req", "exp")),
            P(),
            P(("req", "exp"), None, None),
            P(("req", "exp"), None),
            P(),
            P(),
            P(),
            P(),
            P(),
            P(),
            P(),
            P(),
            P(),
            P(),
            P("exp", None, None),
            P("exp", None, None),
        ),
        out_specs=P(("req", "exp"), None),
        check_vma=False,
    )
```

time: 155 us -> 145 us (0.935)
  the two profiles are of different devices: /device:TPU:1 before, /device:TPU:32 now
where the time goes in v3:
time: 145 us; the launch traced here: 144 us
  Pallas kernels  141 us (97%)
  local copies, waits for them, and re-layouts  3.54 us (2%)
    pallas_call x1, Pallas kernels, layer(): pl.pallas_call(layer_kernel, out_shape=jax.ShapeDtypeStruct((rows, width)...  141 us
    unnamed x2, local copies, waits for them, and re-layouts  3.54 us

profile of v3, /device:TPU:32, one launch (start us, length us, event | category | flops | bytes accessed | tf_op | source)
XLA Modules:
  0.0 144.4 jit_solution(12987082785524363441)
XLA Ops:
  0.0 1.5 %copy.20.routes_ref = s32[256,4]{1,0:T(8,128)} copy(s32[256,4]{0,1:T(4,128)} %param.25) | data formatting | bytes 8192 | tf_op args[6]
  1.5 140.8 %layer.1 = bf16[256,1536]{1,0:T(8,128)(2,1)} custom-call(s32[1,256]{1,0:T(1,128)} %slot_ref.1, s32[4]{0:T(128)} %prompt_ref.1, s32[4]{0:T(128)} %adapter_ref.1, s32[512]{0:T(512)} %table_ref.1, bf16[256,1536]{1,0:T(8,128)(2,1)} %tokens_ref.1, bf16[4,16,512]{2,1,0:T(8,128)(2,1)} %cache_ref.1, bf16[1536]{0:T(1024)(128)(2,1)} %gain_ref.1, ...), custom_call_target="tpu_custom_call" | custom-call | tf_op jit(solution)/shard_map/layer/pallas_call | solution.py:569
  142.3 2.1 %copy.22 = bf16[256,1536]{1,0:T(8,128)(2,1)} copy(bf16[256,1536]{1,0:T(8,128)(2,1)} %layer.1) | data formatting | bytes 1572864

commit v4 on v3

--- a/solution.py
+++ b/solution.py
@@ -30,11 +30,11 @@
 
 
 def layer_kernel(
-    slot_ref, prompt_ref, adapter_ref, table_ref, tokens_ref, cache_ref, gain_ref,
+    slot_ref, prompt_ref, adapter_ref, table_ref, tokens_any, cache_ref, gain_ref,
     routes_ref, expert_gain_ref, router_ref,
     wq_any, wkv_any, aqd_any, aqu_any, wo_any, aod_any, aou_any, wgu_any, wdn_any,
     out_ref,
-    cache, wq, wkv, aqd, aqu, wo, aod, aou, wgu_ref, wdn_ref,
+    cache, tokens_ref, wq, wkv, aqd, aqu, wo, aod, aou, wgu_ref, wdn_ref,
     normed, inner_s, cos_s, sin_s, q_s, k_s, v_s, kv_s, att,
     xbuf, rbuf, rank_s, gate_s, ct_s, arrived, units, returned, psend, precv, acc,
     w_sem, c_sem, ag_s, ag_r, co_s, co_r,
@@ -100,6 +100,8 @@
                 cache.at[x, y, z, c, p * 4 + col], c_sem.at[p * 4 + col])
             cp.start()
             own.append(cp)
+    token_copy = pltpu.make_async_copy(tokens_any, tokens_ref, w_sem.at[9])
+    token_copy.start()
     weights = []
     for i, (src, dst) in enumerate((
             (wkv_any, wkv), (aqd_any, aqd), (aqu_any, aqu), (wq_any, wq),
@@ -214,16 +216,24 @@
     width = tokens_ref.shape[1]
     half_rows = tokens // 2
 
+    for cp in own:
+        cp.wait()
+    pl.semaphore_wait(barrier, 16)
+    for g in groups:
+        ring1[g].begin()
+
+    token_copy.wait()
     tv = tokens_ref[...].astype(jnp.float32)
     factor = lax.rsqrt(jnp.mean(tv * tv, axis=-1, keepdims=True) + EPSILON)
     gain = gain_ref[...].astype(jnp.float32).reshape(1, width)
     normed[...] = (tv * factor * gain).astype(jnp.bfloat16)
 
-    for cp in own:
-        cp.wait()
-    pl.semaphore_wait(barrier, 16)
-    for g in groups:
-        ring1[g].begin()
+    for g in groups:
+        ring1[g].near()
+        ring1[g].finish()
+        ring2[g].begin()
+    for g in groups:
+        ring3[g][0].begin()
 
     slot_row = slot_ref[...]
     index_col = lax.broadcasted_iota(jnp.int32, (tokens, 1), 0).astype(jnp.float32)
@@ -242,32 +252,27 @@
     frequency = jnp.exp(pair * (-math.log(THETA) / (HEAD_WIDTH // 2)))
     angle = position * frequency
     cos_s[...] = jnp.cos(angle)
-    sin_s[...] = jnp.where(lane < HEAD_WIDTH // 2, -jnp.sin(angle), jnp.sin(angle))
 
     def rotate(v):
         return v * cos_s[...] + pltpu.roll(v, HEAD_WIDTH // 2, 1) * sin_s[...]
 
     for g in groups:
-        ring1[g].near()
-        ring1[g].finish()
-        ring2[g].begin()
-    for g in groups:
-        ring3[g][0].begin()
+        ring2[g].near()
+        ring3[g][3].begin()
+        ring3[g][1].begin()
+    for g in groups:
+        ring2[g].finish()
+        ring3[g][2].begin()
+        share_mine(g, 0).start()
+
+    sine = jnp.sin(angle)
+    sin_s[...] = jnp.where(lane < HEAD_WIDTH // 2, -sine, sine)
 
     weights[0].wait()
     kv = jnp.dot(normed[...], wkv[...], preferred_element_type=jnp.float32)
     for h in range(2):
         k_s[h] = rotate(kv[:, h * 128:(h + 1) * 128]).astype(jnp.bfloat16)
         v_s[h] = kv[:, 256 + h * 128:256 + (h + 1) * 128].astype(jnp.bfloat16)
-
-    for g in groups:
-        ring2[g].near()
-        ring3[g][3].begin()
-        ring3[g][1].begin()
-    for g in groups:
-        ring2[g].finish()
-        ring3[g][2].begin()
-        share_mine(g, 0).start()
 
     owner = lax.broadcasted_iota(jnp.int32, (tokens, aqd.shape[1]), 1) // ADAPTER_RANK
     mine = owner == adapter_col
@@ -295,11 +300,8 @@
 
     row_i = lax.broadcasted_iota(jnp.int32, (tokens, tokens), 0)
     col_i = lax.broadcasted_iota(jnp.int32, (tokens, tokens), 1)
-    eye = jnp.where(row_i == col_i, 1.0, 0.0).astype(jnp.bfloat16)
     rbuf[0] = jnp.full(rbuf.shape[1:], -1.0, jnp.float32)
-    rbuf[0, 0:TOPK, :] = lax.dot_general(
-        routes_ref[...].astype(jnp.float32).astype(jnp.bfloat16), eye, (((0,), (0,)), ((), ())),
-        preferred_element_type=jnp.float32)
+    rbuf[0, 0:TOPK, :] = routes_ref[...].astype(jnp.float32)
 
     for o, before in ((3, 0), (1, 3), (2, 1)):
         for g in groups:
@@ -514,25 +516,30 @@
     forward(1).start()
     x_copy(2, 1).wait_recv()
     forward(2).start()
-    for i in (1, 2, 3):
+    for i in (1, 2):
         r_copies[i - 1].wait_recv()
-        if i == 3:
-            forward(1).wait_recv()
-            forward(2).wait_recv()
-        else:
-            x_copy(i, 1 if i == 1 else 0).wait_recv()
+        x_copy(i, 1 if i == 1 else 0).wait_recv()
         make_tables(i)
         dispatch(i)
-        expert(i - 1)
-        if i >= 2:
-            combine(i - 2)
+    expert(1)
+    r_copies[2].wait_recv()
+    forward(1).wait_recv()
+    forward(2).wait_recv()
+    make_tables(3)
+    dispatch(3)
+    expert(2)
     expert(3)
+    combine(1)
+    expert(0)
     combine(2)
     combine(3)
-    for i in (1, 2, 3):
-        partial_copy(i).wait_recv()
-    out_ref[...] = (acc[...] + precv[0].astype(jnp.float32) + precv[1].astype(jnp.float32)
-                    + precv[2].astype(jnp.float32)).astype(jnp.bfloat16)
+    partial_copy(1).wait_recv()
+    acc[...] = acc[...] + precv[0].astype(jnp.float32)
+    combine(0)
+    partial_copy(2).wait_recv()
+    acc[...] = acc[...] + precv[1].astype(jnp.float32)
+    partial_copy(3).wait_recv()
+    out_ref[...] = (acc[...] + precv[2].astype(jnp.float32)).astype(jnp.bfloat16)
     for cp in r_copies:
         cp.wait_send()
     for i in (1, 2):
@@ -569,9 +576,9 @@
     return pl.pallas_call(
         layer_kernel,
         out_shape=jax.ShapeDtypeStruct((rows, width), bf),
-        in_specs=[vmem, smem, smem, smem, vmem, hbm, vmem, vmem, vmem, vmem] + [hbm] * 9,
+        in_specs=[vmem, smem, smem, smem, hbm, hbm, vmem, vmem, vmem, vmem] + [hbm] * 9,
         out_specs=vmem,
-        scratch_shapes=[pltpu.VMEM((4, 4, 4, 2, 16, 16, 128), bf)]
+        scratch_shapes=[pltpu.VMEM((4, 4, 4, 2, 16, 16, 128), bf), pltpu.VMEM((rows, width), bf)]
         + [pltpu.VMEM(w.shape, bf) for w in ordered]
         + [
             pltpu.VMEM((rows, width), bf),
@@ -594,7 +601,7 @@
             pltpu.VMEM((3, rows, width), bf),
             pltpu.VMEM((3, rows, width), bf),
             pltpu.VMEM((rows, width), f32),
-            dma((9,)), dma((16,)), dma((3, 6, 5)), dma((3, 6, 5)), dma((3, 13)), dma((3, 13)),
+            dma((10,)), dma((16,)), dma((3, 6, 5)), dma((3, 6, 5)), dma((3, 13)), dma((3, 13)),
             dma((4, 2)), dma((4, 2)), dma((4,)), dma((4,)),
             dma((4, 8)), dma((4, 8)), dma((4, 8)), dma((4, 8)),
             dma((3,)), dma((3,)),
@@ -602,7 +609,7 @@
         compiler_params=pltpu.CompilerParams(
             collective_id=1, has_side_effects=True, vmem_limit_bytes=63 * 1024 * 1024),
         name="layer",
-    )(slots, prompts, adapters, table, tokens, shard, gain, routes, expert_gain, router.T, *ordered)
+    )(slots, prompts, adapters, table, tokens, shard, gain, routes.T, expert_gain, router.T, *ordered)
 
 
 def on_device(

time: 145 us -> 140 us (0.966)
  the two profiles are of different devices: /device:TPU:32 before, /device:TPU:1 now
where the time goes in v4:
time: 140 us
  Pallas kernels  138 us (99%)
  local copies, waits for them, and re-layouts  2.06 us (1%)
    pallas_call x1, Pallas kernels, layer(): pl.pallas_call(layer_kernel, out_shape=jax.ShapeDtypeStruct((rows, width)...  138 us

profile of v4, /device:TPU:1, one launch (start us, length us, event | category | flops | bytes accessed | tf_op | source)
XLA Modules:
  0.0 139.9 jit_solution(14307735902387027208)
XLA Ops:
  0.0 137.8 %layer.1 = bf16[256,1536]{1,0:T(8,128)(2,1)} custom-call(s32[1,256]{1,0:T(1,128)} %slot_ref.1, s32[4]{0:T(128)} %prompt_ref.1, s32[4]{0:T(128)} %adapter_ref.1, s32[512]{0:T(512)} %table_ref.1, bf16[256,1536]{1,0:T(8,128)(2,1)} %tokens_any.1, bf16[4,16,512]{2,1,0:T(8,128)(2,1)} %cache_ref.1, bf16[1536]{0:T(1024)(128)(2,1)} %gain_ref.1, s32[4,256]{1,0:T(4,128)} %bitcast.7, ...), custom_call_target="tpu_custom_call" | custom-call | tf_op jit(solution)/shard_map/layer/pallas_call | solution.py:576
  137.8 2.1 %copy.21 = bf16[256,1536]{1,0:T(8,128)(2,1)} copy(bf16[256,1536]{1,0:T(8,128)(2,1)} %layer.1) | data formatting | bytes 1572864

commit v5 on v4

--- a/solution.py
+++ b/solution.py
@@ -455,10 +455,15 @@
         return remote(pack.at[pl.ds((i * 8 + q) * CAP, CAP)], arrived.at[i, pl.ds(q * CAP, CAP)],
                       sb_p.at[i, q], rb_p.at[i, q], (x, second_exp(j, dc)))
 
-    def result_copy(i, q):
+    def tile_columns(n):
+        return pl.ds(pl.multiple_of(n * tile, tile), tile)
+
+    def result_copy(i, q, n):
         j, dc = q // 2, q % 2
-        return remote(result.at[pl.ds((i * 8 + q) * CAP, CAP)], returned.at[i, pl.ds(q * CAP, CAP)],
-                      sb_r.at[i, q], rb_r.at[i, q], relay_dev(j, dc))
+        cols = tile_columns(n)
+        return remote(result.at[pl.ds((i * 8 + q) * CAP, CAP), cols],
+                      returned.at[i, pl.ds(q * CAP, CAP), cols],
+                      sb_r.at[i, q, n], rb_r.at[i, q, n], relay_dev(j, dc))
 
     def expert(i):
         for q in range(1, 8):
@@ -479,28 +484,41 @@
             rows = jnp.dot(units[...], wdn_ref[:, cols], preferred_element_type=jnp.float32).astype(jnp.bfloat16)
             returned[i, 0:CAP, cols] = rows[0:CAP]
             result[i * 8 * CAP:(i + 1) * 8 * CAP, cols] = rows
-        for q in range(1, 8):
-            result_copy(i, q).start()
-
-    def partial_copy(i):
-        return remote(psend.at[i - 1], precv.at[i - 1], sp_s.at[i - 1], sp_r.at[i - 1],
-                      first_dev(4 - offsets[i]))
+            for q in range(1, 8):
+                result_copy(i, q, n).start()
+
+    def partial_copy(i, n):
+        cols = tile_columns(n)
+        return remote(psend.at[i - 1, :, cols], precv.at[i - 1, :, cols],
+                      sp_s.at[i - 1, n], sp_r.at[i - 1, n], first_dev(4 - offsets[i]))
+
+    def far_copy(h, n):
+        rows, cols = pl.ds(h * half, half), tile_columns(n)
+        return remote(psend.at[2, rows, cols], precv.at[2, rows, cols],
+                      sp_s.at[2 + h, n], sp_r.at[2 + h, n], first_dev(3 if h == 0 else 1))
 
     def combine(i):
-        for q in range(1, 8):
-            result_copy(i, q).wait_recv()
-
         @pl.loop(0, width // tile)
         def _(n):
-            cols = pl.ds(pl.multiple_of(n * tile, tile), tile)
+            cols = tile_columns(n)
+            for q in range(1, 8):
+                result_copy(i, q, n).wait_recv()
             part = lax.dot_general(ct_s[i], returned[i, :, cols], (((0,), (0,)), ((), ())),
                                    preferred_element_type=jnp.float32)
             if i == 0:
                 acc[:, cols] = acc[:, cols] + part
+            elif i == 3:
+                psend[2, :, cols] = part.astype(jnp.bfloat16)
+                far_copy(0, n).start()
+                far_copy(1, n).start()
             else:
-                psend[i - 1, :, cols] = part.astype(jnp.bfloat16)
-        if i:
-            partial_copy(i).start()
+                rows = slice((i - 1) * half, i * half)
+                rest = slice((2 - i) * half, (3 - i) * half)
+                far_copy(i - 1, n).wait_recv()
+                passed = precv[2, rows, cols].astype(jnp.float32)
+                psend[i - 1, rows, cols] = (part[rows] + passed).astype(jnp.bfloat16)
+                psend[i - 1, rest, cols] = part[rest].astype(jnp.bfloat16)
+                partial_copy(i, n).start()
 
     def forward(i):
         h = 0 if i == 1 else 1
@@ -527,19 +545,26 @@
     forward(2).wait_recv()
     make_tables(3)
     dispatch(3)
+    expert(3)
     expert(2)
-    expert(3)
+    combine(3)
+    expert(0)
     combine(1)
-    expert(0)
     combine(2)
-    combine(3)
-    partial_copy(1).wait_recv()
-    acc[...] = acc[...] + precv[0].astype(jnp.float32)
+    def receive(i):
+        @pl.loop(0, width // tile)
+        def _(n):
+            cols = tile_columns(n)
+            partial_copy(i, n).wait_recv()
+            total = acc[:, cols] + precv[i - 1, :, cols].astype(jnp.float32)
+            if i < 2:
+                acc[:, cols] = total
+            else:
+                out_ref[:, cols] = total.astype(jnp.bfloat16)
+
     combine(0)
-    partial_copy(2).wait_recv()
-    acc[...] = acc[...] + precv[1].astype(jnp.float32)
-    partial_copy(3).wait_recv()
-    out_ref[...] = (acc[...] + precv[2].astype(jnp.float32)).astype(jnp.bfloat16)
+    receive(1)
+    receive(2)
     for cp in r_copies:
         cp.wait_send()
     for i in (1, 2):
@@ -550,9 +575,14 @@
     for i in range(4):
         for q in range(1, 8):
             pack_copy(i, q).wait_send()
-            result_copy(i, q).wait_send()
-        if i:
-            partial_copy(i).wait_send()
+
+        @pl.loop(0, width // tile)
+        def _(n):
+            for q in range(1, 8):
+                result_copy(i, q, n).wait_send()
+            if i in (1, 2):
+                partial_copy(i, n).wait_send()
+                far_copy(i - 1, n).wait_send()
     for g in groups:
         ring1[g].drain()
         ring2[g].drain()
@@ -603,8 +633,8 @@
             pltpu.VMEM((rows, width), f32),
             dma((10,)), dma((16,)), dma((3, 6, 5)), dma((3, 6, 5)), dma((3, 13)), dma((3, 13)),
             dma((4, 2)), dma((4, 2)), dma((4,)), dma((4,)),
-            dma((4, 8)), dma((4, 8)), dma((4, 8)), dma((4, 8)),
-            dma((3,)), dma((3,)),
+            dma((4, 8)), dma((4, 8)), dma((4, 8, 3)), dma((4, 8, 3)),
+            dma((4, 3)), dma((4, 3)),
         ],
         compiler_params=pltpu.CompilerParams(
             collective_id=1, has_side_effects=True, vmem_limit_bytes=63 * 1024 * 1024),

time: 140 us -> 139 us (level)
  Pallas kernels: 138 us -> 136 us
    pallas_call x1, Pallas kernels: 138 us -> 136 us  [layer(): pl.pallas_call(layer_kernel, out_shape=jax.ShapeDtypeStruct((rows, width)...]
where the time goes in v5:
time: 139 us; the launch traced here: 138 us
  Pallas kernels  136 us (98%)
  local copies, waits for them, and re-layouts  2.06 us (1%)
    pallas_call x1, Pallas kernels, layer(): pl.pallas_call(layer_kernel, out_shape=jax.ShapeDtypeStruct((rows, width)...  136 us

profile of v5, /device:TPU:1, one launch (start us, length us, event | category | flops | bytes accessed | tf_op | source)
XLA Modules:
  0.0 138.5 jit_solution(18390409864355651764)
XLA Ops:
  0.0 136.4 %layer.1 = bf16[256,1536]{1,0:T(8,128)(2,1)} custom-call(s32[1,256]{1,0:T(1,128)} %slot_ref.1, s32[4]{0:T(128)} %prompt_ref.1, s32[4]{0:T(128)} %adapter_ref.1, s32[512]{0:T(512)} %table_ref.1, bf16[256,1536]{1,0:T(8,128)(2,1)} %tokens_any.1, bf16[4,16,512]{2,1,0:T(8,128)(2,1)} %cache_ref.1, bf16[1536]{0:T(1024)(128)(2,1)} %gain_ref.1, s32[4,256]{1,0:T(4,128)} %bitcast.7, ...), custom_call_target="tpu_custom_call" | custom-call | tf_op jit(solution)/shard_map/layer/pallas_call | solution.py:606
  136.4 2.1 %copy.21 = bf16[256,1536]{1,0:T(8,128)(2,1)} copy(bf16[256,1536]{1,0:T(8,128)(2,1)} %layer.1) | data formatting | bytes 1572864
